TPU v7x, 32 devices: a whole 2x2x4 slice. The times are simulated.
32 devices in a mesh: gx: 2 (over core), gy: 4 (over z), gz: 4 (over y, x).
Axes of the slice: x: 2, y: 2, z: 4, core: 2. Of those that a mesh axis runs over, the one named last changes fastest.
Arguments:
- particles: float32 [28, 65536], P(None, ('gx', 'gy', 'gz')), may hold values from -3 to 3, as said below
- stencil_base: int32 [3, 65536], P(None, ('gx', 'gy', 'gz')), may hold values from 0 to 32, as said below
- weights: float32 [8, 65536], P(None, ('gx', 'gy', 'gz')), may hold values from 0.02 to 0.25
- gradients: float32 [3, 8, 65536], P(None, None, ('gx', 'gy', 'gz')), may hold values from -4 to 4
- counts: int32 [32], P(('gx', 'gy', 'gz')), may hold values from 0 to 8, as said below
Outputs:
- migrated: float32 [28, 98304], P(None, ('gx', 'gy', 'gz'))
- damage: float32 [16, 64, 128], P('gx', 'gy', 'gz')
Inputs may be any that keep to these rules, and one draw needn't show every extreme that they name: `particles`: mass and volume in 0.5 to 2, deformation gradient entries within 0.1 of the identity's, damage in 0 to 0.5, history in 0.05 to 1. `stencil_base`: row 0 lies in 0 to 8, row 1 in 0 to 16, row 2 in 0 to 32. `counts`: some device hands exactly 8 bins.
All inputs are finite; a program needn't handle non-finite values.
Results may differ from a plain program's by a relative error of at most 0.0003.
Values sent between devices are 32-bit elements; how exact they have to be, the bound alone decides.
A program may use at most 64 MiB of HBM per device.

v0:
```python
import functools
import jax
import jax.numpy as jnp
from jax import lax
from jax.experimental import pallas as pl
from jax.experimental.pallas import tpu as pltpu
from jax.sharding import PartitionSpec as P

CX = 8
CY = 16
CZ = 32
NBIN = 16
BIN = 128
SUBSTEPS = 4
MOST = 8

time_step = 0.1
relax_rate = 0.2
length_sq = 0.6
shear_mod = 1.0
bulk_coef = 1.5
mass_floor = 0.5

MESH = pl.DeviceIdType.MESH


def up_to(value, unit):
    return (value + unit - 1) // unit * unit


H = SUBSTEPS + 1
SX, SY, SZ = CX + 2 * H, CY + 2 * H, CZ + 2 * H
LW = up_to(SY * SZ, 128)
NB = up_to(CY * SZ + CZ + 1, 128)
OFF = (H - 1) * SZ + H - 1
RD = up_to(SX, 8)
DS, VS = SX, CX + 2
DR, VR = up_to(3 * DS, 8), up_to(3 * VS, 16)
XA, XB = (H - 1) * SZ // 128 * 128, up_to((H + 1 + CY) * SZ, 128)
KEEP = H + 1
XROWS = 3 * KEEP + 6
YW = up_to(KEEP * SZ, 128)
YROWS = DR + VR // 2
DT, VT = DR // 8, VR // 8
SLOTS = SZ // KEEP
ZB = (DT + SLOTS - 1) // SLOTS
FOLDS = 3
FW = (CY + 2) // FOLDS * SZ
ZV = up_to(FW, 128)
ZW = ZB * LW + ZV
TAIL = MOST * BIN


def split(value):
    high = value.astype(jnp.bfloat16)
    low = (value - high.astype(jnp.float32)).astype(jnp.bfloat16)
    return high, low


def take(ref, lane0, width):
    a = lane0 // 128 * 128
    span = up_to(lane0 - a + width, 128)
    value = ref[:, a : a + span]
    shift = (span - (lane0 - a)) % span
    if shift:
        value = pltpu.roll(value, shift, 1)
    value = value[:, : up_to(width, 128)]
    lane = lax.broadcasted_iota(jnp.int32, value.shape, 1)
    return jnp.where(lane < width, value, 0.0)


def put_add(ref, lane0, width, value):
    a = lane0 // 128 * 128
    span = max(up_to(lane0 - a + width, 128), value.shape[1])
    extra = span - value.shape[1]
    if extra:
        value = jnp.concatenate([value, jnp.zeros((value.shape[0], extra), jnp.float32)], axis=1)
    if lane0 - a:
        value = pltpu.roll(value, lane0 - a, 1)
    ref[:, a : a + span] += value


def make_onehot(base_ref, hot):
    flat = base_ref[1:2, :] * SZ + base_ref[2:3, :]
    for r in range(0, NB, 128):
        row = lax.broadcasted_iota(jnp.int32, (128, flat.shape[1]), 0) + r
        hot[r : r + 128, :] = (row == flat).astype(jnp.float32).astype(jnp.bfloat16)


def scatter(part, base_ref, weight, slope, hot, coef, left, nodes, dref, vref, xs_low, xs_high):
    count = part.shape[1]
    mass = part[0:1, :]
    scale = -time_step * part[1:2, :]
    coef[...] = jnp.zeros_like(coef)
    coef[0:1, :] = mass
    coef[1:2, :] = mass * part[23:24, :]
    coef[2:3, :] = mass * part[24:25, :]
    coef[3:6, :] = mass * part[2:5, :]
    for j in range(3):
        for i in range(3):
            coef[8 + 8 * j + 3 + i : 8 + 8 * j + 4 + i, :] = scale * part[14 + 3 * i + j : 15 + 3 * i + j, :]
    bx = jnp.broadcast_to(base_ref[0:1, :], (8, count))
    for bc in range(4):
        pair = []
        for a in range(2):
            k = 4 * a + bc
            term = weight[k : k + 1, :] * coef[0:8, :]
            for j in range(3):
                term = term + slope[8 * j + k : 8 * j + k + 1, :] * coef[8 + 8 * j : 16 + 8 * j, :]
            high = term.astype(jnp.bfloat16).astype(jnp.float32)
            pair.append((high, term - high))
        for x in range(CX + 2):
            for s in range(2):
                row = x * 64 + s * 32 + bc * 8
                value = jnp.where(bx == x, pair[0][s], jnp.where(bx == x - 1, pair[1][s], 0.0))
                left[row : row + 8, :] = value.astype(jnp.bfloat16)
    sums = lax.dot_general(left[...], hot[...], (((1,), (1,)), ((), ())), preferred_element_type=jnp.float32)
    sums = sums.reshape(CX + 2, 2, 4, 8, NB)
    sums = sums[:, 0] + sums[:, 1]
    total = None
    for bc in range(4):
        piece = sums[:, bc].reshape((CX + 2) * 8, NB)
        piece = jnp.concatenate([piece, jnp.zeros((piece.shape[0], LW - NB), jnp.float32)], axis=1)
        piece = pltpu.roll(piece, OFF + (bc >> 1) * SZ + (bc & 1), 1)
        total = piece if total is None else total + piece
    for x in range(CX + 2):
        nodes[x] = total[8 * x : 8 * x + 8, :]
    dref[...] = jnp.zeros_like(dref)
    vref[...] = jnp.zeros_like(vref)
    for x in range(CX + 2):
        for c in range(3):
            dref[c * DS + H - 1 + x : c * DS + H + x, :] = nodes[x, c : c + 1, :]
            vref[c * VS + x : c * VS + x + 1, :] = nodes[x, 3 + c : 4 + c, :]
    for c in range(3):
        at = c * DS + H - 1
        xs_high[c * KEEP : (c + 1) * KEEP, :] = dref[at + CX + 2 - KEEP : at + CX + 2, XA:XB]
        xs_low[c * KEEP : (c + 1) * KEEP, :] = dref[at : at + KEEP, XA:XB]
        at = 3 * KEEP + 2 * c
        xs_high[at : at + 2, :] = vref[c * VS + CX : c * VS + CX + 2, XA:XB]
        xs_low[at : at + 2, :] = vref[c * VS : c * VS + 2, XA:XB]


def only(has, value):
    return jnp.where(has, value, jnp.zeros_like(value))


def add_x(dref, vref, from_low, from_high, has_low, has_high, ys_low, ys_high):
    low = only(has_low, from_low[...])
    high = only(has_high, from_high[...])
    for c in range(3):
        dref[c * DS : c * DS + KEEP, XA:XB] += low[c * KEEP : (c + 1) * KEEP]
        dref[c * DS + SX - KEEP : c * DS + SX, XA:XB] += high[c * KEEP : (c + 1) * KEEP]
        at = 3 * KEEP + 2 * c
        vref[c * VS : c * VS + 2, XA:XB] += low[at : at + 2]
        vref[c * VS + CX : c * VS + CX + 2, XA:XB] += high[at : at + 2]
    half = VR // 2
    for ys, d0, v0 in ((ys_high, CY * SZ, (H - 1 + CY) * SZ), (ys_low, (H - 1) * SZ, (H - 1) * SZ)):
        ys[:DR, :] = take(dref.at[:DR], d0, KEEP * SZ)
        near = take(vref, v0, 2 * SZ)
        ys[DR:, 0:128] = near[:half]
        ys[DR:, 128:256] = near[half:]


def lane_z():
    lane = lax.broadcasted_iota(jnp.int32, (8, LW), 1).astype(jnp.float32)
    y = jnp.floor((lane + 0.5) * (1.0 / SZ))
    return lane - SZ * y, y


def in_slot(z, at, width):
    return (z >= at) & (z < at + width)


def spin(value, shift):
    shift = shift % value.shape[1]
    return pltpu.roll(value, shift, 1) if shift else value


def add_y(dref, vref, from_low, from_high, has_low, has_high, zs_low, zs_high):
    for got, has, d0, v0 in (
        (from_low, has_low, 0, (H - 1) * SZ),
        (from_high, has_high, (SY - KEEP) * SZ, (H - 1 + CY) * SZ),
    ):
        put_add(dref.at[:DR], d0, KEEP * SZ, only(has, got[:DR, :]))
        near = jnp.concatenate([got[DR:, 0:128], got[DR:, 128:256]], axis=0)
        put_add(vref, v0, 2 * SZ, only(has, near))
    z, _ = lane_z()
    short = z[:, :ZV]
    for zs, d0, v0 in ((zs_high, CZ, H - 1 + CZ), (zs_low, H - 1, H - 1)):
        for block in range(ZB):
            out = jnp.zeros((8, LW), jnp.float32)
            for s in range(min(SLOTS, DT - block * SLOTS)):
                r = 8 * (block * SLOTS + s)
                value = spin(dref[r : r + 8, :], s * KEEP - d0)
                out = jnp.where(in_slot(z, s * KEEP, KEEP), value, out)
            zs[:, block * LW : (block + 1) * LW] = out
        out = jnp.zeros((8, ZV), jnp.float32)
        for t in range(VT):
            for q in range(FOLDS):
                at = 2 * (t * FOLDS + q)
                value = take(vref.at[8 * t : 8 * t + 8], (H - 1) * SZ + q * FW + v0, FW)
                value = spin(value, at)
                out = jnp.where(in_slot(short, at, 2), value, out)
        zs[:, ZB * LW :] = out


def add_z(dref, vref, from_low, from_high, has_low, has_high):
    z, _ = lane_z()
    short = z[:, :ZV]
    lane = lax.broadcasted_iota(jnp.int32, (8, ZV), 1)
    for got, has, d0, v0 in (
        (from_low, has_low, 0, H - 1),
        (from_high, has_high, SZ - KEEP, H - 1 + CZ),
    ):
        for block in range(ZB):
            whole = only(has, got[:, block * LW : (block + 1) * LW])
            for s in range(min(SLOTS, DT - block * SLOTS)):
                r = 8 * (block * SLOTS + s)
                value = jnp.where(in_slot(z, s * KEEP, KEEP), whole, 0.0)
                dref[r : r + 8, :] += spin(value, d0 - s * KEEP)
        whole = only(has, got[:, ZB * LW :])
        for t in range(VT):
            for q in range(FOLDS):
                at = 2 * (t * FOLDS + q)
                value = jnp.where(in_slot(short, at, 2) & (lane < FW), whole, 0.0)
                value = spin(value, -at)
                put_add(vref.at[8 * t : 8 * t + 8], (H - 1) * SZ + q * FW + v0, FW, value)


def relax_all(dref, vref, place, nodes_x, nodes_y, nodes_z, wet, fields, field_left, damage_out):
    ix, iy, iz = place
    z, y = lane_z()
    z, y = z[0:1], y[0:1]
    gz = z - H + (iz * CZ).astype(jnp.float32)
    gy = y - H + (iy * CY).astype(jnp.float32)
    flat_in = (gz >= 0) & (gz < nodes_z) & (gy >= 0) & (gy < nodes_y) & (y < SY)
    row = lax.broadcasted_iota(jnp.int32, (RD, 1), 0)
    gx = row - H + ix * CX
    row_in = (gx >= 0) & (gx < nodes_x) & (row < SX)
    inside = row_in.astype(jnp.float32) * flat_in.astype(jnp.float32)
    mass = jnp.maximum(dref[0:RD, :], mass_floor)
    damage = dref[DS : DS + RD, :] / mass * inside
    drive = dref[2 * DS : 2 * DS + RD, :] / mass
    wet[0:RD, :] = mass
    wet[RD : 2 * RD, :] = inside
    for _ in range(SUBSTEPS):
        ring = (
            pltpu.roll(damage, 1, 0)
            + pltpu.roll(damage, RD - 1, 0)
            + pltpu.roll(damage, SZ, 1)
            + pltpu.roll(damage, LW - SZ, 1)
            + pltpu.roll(damage, 1, 1)
            + pltpu.roll(damage, LW - 1, 1)
        )
        laplace = ring - 6.0 * damage
        damage = (damage + relax_rate * (length_sq * laplace - damage + 2.0 * (1.0 - damage) * drive)) * inside
    wet[2 * RD : 3 * RD, :] = damage
    damage_out[...] = wet[2 * RD + H : 2 * RD + H + CX, :]
    n = CX + 2
    factor = wet[RD + H - 1 : RD + H - 1 + n, :] / wet[H - 1 : H - 1 + n, :]
    fields[...] = jnp.zeros_like(fields)
    for c in range(3):
        fields[c * 16 : c * 16 + n, :] = vref[c * VS : c * VS + n, :] * factor
    fields[48 : 48 + n, :] = wet[2 * RD + H - 1 : 2 * RD + H - 1 + n, :]
    whole = fields[...]
    for bc in range(4):
        moved = pltpu.roll(whole, LW - OFF - (bc >> 1) * SZ - (bc & 1), 1)[:, :NB]
        for f in range(4):
            for x in range(n):
                r = x * 16 + f * 4 + bc
                field_left[r : r + 1, :] = moved[f * 16 + x : f * 16 + x + 1, :]


def advance(part, base_ref, weight, slope, hot, field_left, out, at, count):
    lanes = slice(at, at + count)
    there = slice(TAIL + at, TAIL + at + count)
    n = CX + 2
    high, low = split(field_left[...])
    got = jnp.dot(high, hot[:, lanes], preferred_element_type=jnp.float32)
    got = got + jnp.dot(low, hot[:, lanes], preferred_element_type=jnp.float32)
    bx = jnp.broadcast_to(base_ref[0:1, lanes], (16, count))
    near = [jnp.zeros((16, count), jnp.float32), jnp.zeros((16, count), jnp.float32)]
    for x in range(n):
        rows = got[16 * x : 16 * x + 16]
        near[0] = jnp.where(bx == x, rows, near[0])
        near[1] = jnp.where(bx == x - 1, rows, near[1])
    w = weight[:, lanes]
    g = [slope[8 * j : 8 * j + 8, lanes] for j in range(3)]
    corner = [jnp.concatenate([near[0][4 * f : 4 * f + 4], near[1][4 * f : 4 * f + 4]], axis=0) for f in range(4)]
    total = lambda v: jnp.sum(v, axis=0, keepdims=True)
    moved = [total(w * corner[i]) for i in range(3)]
    velgrad = [[total(corner[i] * g[j]) for j in range(3)] for i in range(3)]
    damage_node = total(w * corner[3])
    p = lambda r: part[r : r + 1, lanes]
    deform = [[p(5 + 3 * i + j) for j in range(3)] for i in range(3)]
    stretch = [[(1.0 if i == j else 0.0) + time_step * velgrad[i][j] for j in range(3)] for i in range(3)]
    mapped = [
        [stretch[i][0] * deform[0][j] + stretch[i][1] * deform[1][j] + stretch[i][2] * deform[2][j] for j in range(3)]
        for i in range(3)
    ]
    jacobian = (
        mapped[0][0] * (mapped[1][1] * mapped[2][2] - mapped[1][2] * mapped[2][1])
        - mapped[0][1] * (mapped[1][0] * mapped[2][2] - mapped[1][2] * mapped[2][0])
        + mapped[0][2] * (mapped[1][0] * mapped[2][1] - mapped[1][1] * mapped[2][0])
    )
    left = {}
    for i in range(3):
        for j in range(i, 3):
            left[i, j] = mapped[i][0] * mapped[j][0] + mapped[i][1] * mapped[j][1] + mapped[i][2] * mapped[j][2]
            left[j, i] = left[i, j]
    damaged = jnp.maximum(p(23), damage_node)
    degrade = (1.0 - damaged) ** 2
    swell = bulk_coef * (jacobian - 1.0)

    def put(r, value):
        out[r : r + 1, there] = value

    out[0:2, there] = part[0:2, lanes]
    for i in range(3):
        put(2 + i, moved[i])
        put(25 + i, p(25 + i) + time_step * moved[i])
        for j in range(3):
            put(5 + 3 * i + j, mapped[i][j])
            term = shear_mod * (left[i, j] - (1.0 if i == j else 0.0))
            if i == j:
                term = term + swell
            put(14 + 3 * i + j, degrade * term)
    put(23, damaged)
    energy = 0.5 * shear_mod * (left[0, 0] + left[1, 1] + left[2, 2] - 3.0) + 0.5 * bulk_coef * (jacobian - 1.0) ** 2
    put(24, jnp.maximum(p(24), energy))


def step_kernel(
    sizes, part, base_ref, weight, slope, counts, migrated, damage_out,
    hot, coef, left, nodes, dref, vref, wet, fields, field_left,
    sx, rx, sy, ry, sz, rz, ext, tell, told, send_sem, recv_sem,
):
    names = ("gx", "gy", "gz")
    place = [lax.axis_index(a) for a in names]
    has_low = [i > 0 for i in place]
    has_high = [i < n - 1 for i, n in zip(place, sizes)]
    last = sizes[2]
    following, previous = lax.rem(place[2] + 1, last), lax.rem(place[2] + last - 1, last)
    barrier = pltpu.get_barrier_semaphore()
    waits = 2
    for k in range(2):
        for has, other in ((has_low[k], place[k] - 1), (has_high[k], place[k] + 1)):
            @pl.when(has)
            def _(k=k, other=other):
                pl.semaphore_signal(barrier, inc=1, device_id={names[k]: other}, device_id_type=MESH)
            waits = waits + has.astype(jnp.int32)
    for other in (following, previous):
        pl.semaphore_signal(barrier, inc=1, device_id={"gz": other}, device_id_type=MESH)

    make_onehot(base_ref, hot)
    scatter(part, base_ref, weight, slope, hot, coef, left, nodes, dref, vref, sx.at[0], sx.at[1])
    pl.semaphore_wait(barrier, waits)

    def copies(k, src, dst):
        made = []
        for d, other in ((0, place[k] - 1), (1, place[k] + 1)):
            made.append(pltpu.make_async_remote_copy(
                src_ref=src.at[d], dst_ref=dst.at[1 - d], send_sem=send_sem.at[k, d],
                recv_sem=recv_sem.at[k, 1 - d], device_id={names[k]: other}, device_id_type=MESH))
        return made

    def exchange(k, src, dst):
        made = copies(k, src, dst)
        ahead = ((has_low[k], made[0]), (has_high[k], made[1]))
        for has, copy in ahead:
            @pl.when(has)
            def _(copy=copy):
                copy.start()
        for has, copy in ((has_low[k], made[1]), (has_high[k], made[0])):
            @pl.when(has)
            def _(copy=copy):
                copy.wait_recv()
        for has, copy in ahead:
            @pl.when(has)
            def _(copy=copy):
                copy.wait_send()

    exchange(0, sx, rx)
    add_x(dref, vref, rx.at[0], rx.at[1], has_low[0], has_high[0], sy.at[0], sy.at[1])
    exchange(1, sy, ry)
    add_y(dref, vref, ry.at[0], ry.at[1], has_low[1], has_high[1], sz.at[0], sz.at[1])
    exchange(2, sz, rz)
    add_z(dref, vref, rz.at[0], rz.at[1], has_low[2], has_high[2])
    relax_all(dref, vref, place, sizes[0] * CX, sizes[1] * CY, sizes[2] * CZ, wet, fields, field_left, damage_out)
    count = part.shape[1]

    def to_next(src, dst, slot):
        copy = pltpu.make_async_remote_copy(
            src_ref=src, dst_ref=dst, send_sem=send_sem.at[3 + slot, 0], recv_sem=recv_sem.at[3 + slot, 0],
            device_id={"gz": following}, device_id_type=MESH)
        copy.start()
        return copy

    tell[...] = jnp.broadcast_to(counts[0], tell.shape)
    flying = [to_next(tell, told, 0)]
    chunk = TAIL // 2
    for k in (1, 0):
        at = count - TAIL + k * chunk
        advance(part, base_ref, weight, slope, hot, field_left, ext, at, chunk)
        flying.append(to_next(ext.at[:, TAIL + at : TAIL + at + chunk], ext.at[:, k * chunk : (k + 1) * chunk], 1 + k))
    for at in range(0, count - TAIL, chunk):
        advance(part, base_ref, weight, slope, hot, field_left, ext, at, min(chunk, count - TAIL - at))
    ext[:, TAIL + count :] = jnp.zeros((28, TAIL), jnp.float32)
    for copy in flying:
        copy.wait()
    prior = jnp.broadcast_to(told[0:1, :], (28, BIN))
    live = prior + jnp.broadcast_to(count // BIN - counts[0], prior.shape)
    block = lambda j: ext[:, j * BIN : (j + 1) * BIN]
    for j in range(count // BIN + MOST):
        piece = block(MOST + j)
        for p in range(1, MOST + 1):
            piece = jnp.where(prior == p, block(MOST - p + j), piece)
        migrated[:, j * BIN : (j + 1) * BIN] = jnp.where(live > j, piece, 0.0)


def per_device(particles, stencil_base, weights, gradients, counts):
    count = particles.shape[1]
    sizes = tuple(lax.axis_size(a) for a in ("gx", "gy", "gz"))
    vmem = pl.BlockSpec(memory_space=pltpu.VMEM)
    f32 = jnp.float32
    migrated, flat_damage = pl.pallas_call(
        functools.partial(step_kernel, sizes),
        name="step",
        out_shape=(
            jax.ShapeDtypeStruct((28, count + TAIL), f32),
            jax.ShapeDtypeStruct((CX, LW), f32),
        ),
        in_specs=[vmem] * 4 + [pl.BlockSpec(memory_space=pltpu.SMEM)],
        out_specs=(vmem,) * 2,
        scratch_shapes=[
            pltpu.VMEM((NB, count), jnp.bfloat16),
            pltpu.VMEM((32, count), f32),
            pltpu.VMEM(((CX + 2) * 64, count), jnp.bfloat16),
            pltpu.VMEM((CX + 2, 8, LW), f32),
            pltpu.VMEM((up_to(2 * DS + RD, 8), LW), f32),
            pltpu.VMEM((VR, LW), f32),
            pltpu.VMEM((3 * RD, LW), f32),
            pltpu.VMEM((64, LW), f32),
            pltpu.VMEM(((CX + 2) * 16, NB), f32),
            pltpu.VMEM((2, XROWS, XB - XA), f32),
            pltpu.VMEM((2, XROWS, XB - XA), f32),
            pltpu.VMEM((2, YROWS, YW), f32),
            pltpu.VMEM((2, YROWS, YW), f32),
            pltpu.VMEM((2, 8, ZW), f32),
            pltpu.VMEM((2, 8, ZW), f32),
            pltpu.VMEM((28, count + 2 * TAIL), f32),
            pltpu.VMEM((8, 128), jnp.int32),
            pltpu.VMEM((8, 128), jnp.int32),
            pltpu.SemaphoreType.DMA((6, 2)),
            pltpu.SemaphoreType.DMA((6, 2)),
        ],
        compiler_params=pltpu.CompilerParams(
            collective_id=0, has_side_effects=True, vmem_limit_bytes=60 * 1024 * 1024
        ),
    )(particles, stencil_base, weights, gradients.reshape(24, count), counts)
    damage = flat_damage[:, : SY * SZ].reshape(CX, SY, SZ)[:, H : H + CY, H : H + CZ]
    return (migrated, damage)


def solution(mesh):
    return jax.shard_map(
        per_device,
        mesh=mesh,
        in_specs=(
            P(None, ("gx", "gy", "gz")),
            P(None, ("gx", "gy", "gz")),
            P(None, ("gx", "gy", "gz")),
            P(None, None, ("gx", "gy", "gz")),
            P(("gx", "gy", "gz")),
        ),
        out_specs=(P(None, ("gx", "gy", "gz")), P("gx", "gy", "gz")),
        check_vma=False,
    )
```

profile of v0, /device:TPU:0, one launch (start us, length us, event | category | flops | bytes accessed | tf_op | source)
XLA Modules:
  0.0 28.7 jit_solution(10757586679575779244)
XLA Ops:
  1.3 24.0 %step.1 = (f32[28,3072]{1,0:T(8,128)}, f32[8,1152]{1,0:T(8,128)}) custom-call(f32[28,2048]{1,0:T(8,128)} %part.1, s32[3,2048]{1,0:T(4,128)} %base_ref.1, f32[8,2048]{1,0:T(8,128)} %weight.1, f32[24,2048]{1,0:T(8,128)} %bitcast.2, s32[1]{0:T(128)S(6)} %copy.8.counts), custom_call_target="tpu_custom_call" | custom-call | tf_op jit(solution)/shard_map/step/pallas_call | solution.py:426
  25.2 0.9 %reshape.11 = f32[8,26,42]{2,1,0:T(8,128)S(1)} reshape(f32[8,1092]{1,0:T(8,128)} %bitcast.3) | data formatting | bytes 69888 | tf_op jit(solution)/shard_map/reshape | solution.py:461
  26.2 0.7 %slice.8 = f32[8,16,32]{2,1,0:T(8,128)} slice(f32[8,26,42]{2,1,0:T(8,128)S(1)} %reshape.11), slice={[0:8], [5:21], [5:37]} | slice | bytes 32768 | tf_op jit(solution)/shard_map/slice | solution.py:461
  26.9 1.8 %copy.9 = f32[28,3072]{1,0:T(8,128)} copy(f32[28,3072]{1,0:T(8,128)} %get-tuple-element.8) | data formatting | bytes 688128
where the time goes:
time: 28.9 us; the launch traced here: 28.7 us
  Pallas kernels  24 us (83%)
  local copies, waits for them, and re-layouts  3.4 us (12%)
  between operations  1.29 us (4%)
    pallas_call x1, Pallas kernels, per_device(): pl.pallas_call(functools.partial(step_kernel, sizes), name='step', out_sh...  24 us
    unnamed x1, local copies, waits for them, and re-layouts  1.77 us
    reshape x1, local copies, waits for them, and re-layouts, per_device(): damage = flat_damage[:, :SY * SZ].reshape(CX, SY, SZ)[:, H:H + CY, H:H + CZ]  0.92 us
    slice x1, local copies, waits for them, and re-layouts, per_device(): damage = flat_damage[:, :SY * SZ].reshape(CX, SY, SZ)[:, H:H + CY, H:H + CZ]  0.72 us

commit v1 on v0

--- a/solution.py
+++ b/solution.py
@@ -255,7 +255,9 @@
         laplace = ring - 6.0 * damage
         damage = (damage + relax_rate * (length_sq * laplace - damage + 2.0 * (1.0 - damage) * drive)) * inside
     wet[2 * RD : 3 * RD, :] = damage
-    damage_out[...] = wet[2 * RD + H : 2 * RD + H + CX, :]
+    own = wet[2 * RD + H : 2 * RD + H + CX, :]
+    for y in range(CY):
+        damage_out[:, y, :] = pltpu.roll(own, LW - (H + y) * SZ - H, 1)[:, :CZ]
     n = CX + 2
     factor = wet[RD + H - 1 : RD + H - 1 + n, :] / wet[H - 1 : H - 1 + n, :]
     fields[...] = jnp.zeros_like(fields)
@@ -331,9 +333,9 @@
 
 
 def step_kernel(
-    sizes, part, base_ref, weight, slope, counts, migrated, damage_out,
+    sizes, part, base_ref, weight, slope, counts, ext, prior_out, damage_out,
     hot, coef, left, nodes, dref, vref, wet, fields, field_left,
-    sx, rx, sy, ry, sz, rz, ext, tell, told, send_sem, recv_sem,
+    sx, rx, sy, ry, sz, rz, tell, told, send_sem, recv_sem,
 ):
     names = ("gx", "gy", "gz")
     place = [lax.axis_index(a) for a in names]
@@ -408,14 +410,24 @@
     ext[:, TAIL + count :] = jnp.zeros((28, TAIL), jnp.float32)
     for copy in flying:
         copy.wait()
-    prior = jnp.broadcast_to(told[0:1, :], (28, BIN))
-    live = prior + jnp.broadcast_to(count // BIN - counts[0], prior.shape)
-    block = lambda j: ext[:, j * BIN : (j + 1) * BIN]
-    for j in range(count // BIN + MOST):
-        piece = block(MOST + j)
-        for p in range(1, MOST + 1):
-            piece = jnp.where(prior == p, block(MOST - p + j), piece)
-        migrated[:, j * BIN : (j + 1) * BIN] = jnp.where(live > j, piece, 0.0)
+    prior_out[...] = told[...]
+    for j in range(count // BIN - MOST, count // BIN):
+        gone = jnp.broadcast_to(counts[0], (28, BIN)) >= count // BIN - j
+        lanes = slice(TAIL + j * BIN, TAIL + (j + 1) * BIN)
+        ext[:, lanes] = jnp.where(gone, 0.0, ext[:, lanes])
+
+
+def place_kernel(ext, prior_ref, damage_in, migrated, damage_out, sem):
+    width = migrated.shape[1]
+    start = pl.multiple_of((MOST - prior_ref[0, 0]) * BIN, BIN)
+    copies = [
+        pltpu.make_async_copy(ext.at[:, pl.ds(start, width)], migrated, sem.at[0]),
+        pltpu.make_async_copy(damage_in, damage_out, sem.at[1]),
+    ]
+    for copy in copies:
+        copy.start()
+    for copy in copies:
+        copy.wait()
 
 
 def per_device(particles, stencil_base, weights, gradients, counts):
@@ -423,15 +435,16 @@
     sizes = tuple(lax.axis_size(a) for a in ("gx", "gy", "gz"))
     vmem = pl.BlockSpec(memory_space=pltpu.VMEM)
     f32 = jnp.float32
-    migrated, flat_damage = pl.pallas_call(
+    ext, prior, near_damage = pl.pallas_call(
         functools.partial(step_kernel, sizes),
         name="step",
         out_shape=(
-            jax.ShapeDtypeStruct((28, count + TAIL), f32),
-            jax.ShapeDtypeStruct((CX, LW), f32),
+            pltpu.VMEM((28, count + 2 * TAIL), f32),
+            pltpu.VMEM((8, 128), jnp.int32),
+            pltpu.VMEM((CX, CY, CZ), f32),
         ),
         in_specs=[vmem] * 4 + [pl.BlockSpec(memory_space=pltpu.SMEM)],
-        out_specs=(vmem,) * 2,
+        out_specs=(vmem,) * 3,
         scratch_shapes=[
             pltpu.VMEM((NB, count), jnp.bfloat16),
             pltpu.VMEM((32, count), f32),
@@ -448,7 +461,6 @@
             pltpu.VMEM((2, YROWS, YW), f32),
             pltpu.VMEM((2, 8, ZW), f32),
             pltpu.VMEM((2, 8, ZW), f32),
-            pltpu.VMEM((28, count + 2 * TAIL), f32),
             pltpu.VMEM((8, 128), jnp.int32),
             pltpu.VMEM((8, 128), jnp.int32),
             pltpu.SemaphoreType.DMA((6, 2)),
@@ -458,8 +470,18 @@
             collective_id=0, has_side_effects=True, vmem_limit_bytes=60 * 1024 * 1024
         ),
     )(particles, stencil_base, weights, gradients.reshape(24, count), counts)
-    damage = flat_damage[:, : SY * SZ].reshape(CX, SY, SZ)[:, H : H + CY, H : H + CZ]
-    return (migrated, damage)
+    return pl.pallas_call(
+        place_kernel,
+        name="place",
+        out_shape=(
+            jax.ShapeDtypeStruct((28, count + TAIL), f32),
+            jax.ShapeDtypeStruct((CX, CY, CZ), f32),
+        ),
+        in_specs=[pl.BlockSpec(memory_space=pl.ANY), pl.BlockSpec(memory_space=pltpu.VMEM), pl.BlockSpec(memory_space=pl.ANY)],
+        out_specs=(pl.BlockSpec(memory_space=pl.ANY),) * 2,
+        scratch_shapes=[pltpu.SemaphoreType.DMA((2,))],
+        compiler_params=pltpu.CompilerParams(vmem_limit_bytes=4 * 1024 * 1024),
+    )(ext, prior, near_damage)
 
 
 def solution(mesh):

time: 28.9 us -> 25.4 us (0.88)
  local copies, waits for them, and re-layouts: 3.4 us -> 0 us
    unnamed x1 -> x0, local copies, waits for them, and re-layouts: 1.77 us -> none
    reshape x1 -> x0, local copies, waits for them, and re-layouts: 0.92 us -> none  [per_device(): damage = flat_damage[:, :SY * SZ].reshape(CX, SY, SZ)[:, H:H + CY, H:H + CZ]]
    pallas_call x1, Pallas kernels: 24 us -> 23.1 us  [per_device(): pl.pallas_call(functools.partial(step_kernel, sizes), name='step', out_sh...]
    pallas_call x0 -> x1, Pallas kernels: none -> 0.81 us  [per_device(): pl.pallas_call(place_kernel, name='place', out_shape=(jax.ShapeDtypeStruc...]
    slice x1 -> x0, local copies, waits for them, and re-layouts: 0.72 us -> none  [per_device(): damage = flat_damage[:, :SY * SZ].reshape(CX, SY, SZ)[:, H:H + CY, H:H + CZ]]
where the time goes in v1:
time: 25.4 us; the launch traced here: 25.2 us
  Pallas kernels  23.9 us (94%)
  between operations  1.29 us (5%)
    pallas_call x1, Pallas kernels, per_device(): pl.pallas_call(functools.partial(step_kernel, sizes), name='step', out_sh...  23.1 us
    pallas_call x1, Pallas kernels, per_device(): pl.pallas_call(place_kernel, name='place', out_shape=(jax.ShapeDtypeStruc...  0.81 us

profile of v1, /device:TPU:0, one launch (start us, length us, event | category | flops | bytes accessed | tf_op | source)
XLA Modules:
  0.0 25.2 jit_solution(11835261551388352177)
XLA Ops:
  1.3 23.1 %step.1 = (f32[28,4096]{1,0:T(8,128)S(1)}, s32[8,128]{1,0:T(8,128)S(1)}, f32[8,16,32]{2,1,0:T(8,128)S(1)}) custom-call(f32[28,2048]{1,0:T(8,128)} %part.1, s32[3,2048]{1,0:T(4,128)} %base_ref.1, f32[8,2048]{1,0:T(8,128)} %weight.1, f32[24,2048]{1,0:T(8,128)} %bitcast.1, s32[1]{0:T(128)S(6)} %copy.7.counts), custom_call_target="tpu_custom_call" | custom-call | tf_op jit(solution)/shard_map/step/pallas_call | solution.py:438
  24.4 0.8 %place.1 = (f32[28,3072]{1,0:T(8,128)}, f32[8,16,32]{2,1,0:T(8,128)}) custom-call(f32[28,4096]{1,0:T(8,128)S(1)} %get-tuple-element.5.ext, s32[8,128]{1,0:T(8,128)S(1)} %get-tuple-element.6.prior_ref, f32[8,16,32]{2,1,0:T(8,128)S(1)} %get-tuple-element.7.damage_in), custom_call_target="tpu_custom_call" | custom-call | tf_op jit(solution)/shard_map/place/pallas_call | solution.py:473

commit v2 on v1

v2 whole, which is shorter than its diff:
```python
import functools
import jax
import jax.numpy as jnp
from jax import lax
from jax.experimental import pallas as pl
from jax.experimental.pallas import tpu as pltpu
from jax.sharding import PartitionSpec as P

CX = 8
CY = 16
CZ = 32
NBIN = 16
BIN = 128
SUBSTEPS = 4
MOST = 8

time_step = 0.1
relax_rate = 0.2
length_sq = 0.6
shear_mod = 1.0
bulk_coef = 1.5
mass_floor = 0.5

MESH = pl.DeviceIdType.MESH


def up_to(value, unit):
    return (value + unit - 1) // unit * unit


H = SUBSTEPS + 1
EX, EY, EZ = CX + 2, CY + 2, CZ + 2
SX, SY, SZ = CX + 2 * H, CY + 2 * H, CZ + 2 * H
LANE = 128
LW = up_to(SY * SZ, LANE)
NB = up_to((CY + 1) * SZ + CZ + 2, LANE)
JB = NB // LANE
OFF = (H - 1) * SZ + H - 1
KEEP = H + 1
RD = 24
ROWS = 32
LEFT = EX * 24
PATTERNS = 3
WIDE = {0: KEEP, 1: 2}
FACE = {0: up_to(KEEP * SZ, LANE), 1: up_to(2 * SZ, LANE)}
ZA, ZB = (H - 1) * SZ // LANE * LANE, up_to((H + CY + 1) * SZ, LANE)
FL = EX * 16
TAIL = MOST * BIN
PARTS = 28
SLOT = 32
GROUPS = 8
LATE = 13
EARLY = 7
DIRS = [(dy, dz) for dy in (-1, 0, 1) for dz in (-1, 0, 1) if (dy, dz) != (0, 0)]


def iota(shape, axis):
    return lax.broadcasted_iota(jnp.int32, shape, axis)


def take(value, lane0, width):
    a = lane0 // LANE * LANE
    span = up_to(lane0 - a + width, LANE)
    value = value[:, a : a + span]
    shift = (span - (lane0 - a)) % span
    if shift:
        value = pltpu.roll(value, shift, 1)
    value = value[:, : up_to(width, LANE)]
    return jnp.where(iota(value.shape, 1) < width, value, 0.0)


def put_add(ref, lane0, width, value):
    a = lane0 // LANE * LANE
    span = max(up_to(lane0 - a + width, LANE), value.shape[1])
    extra = span - value.shape[1]
    if extra:
        value = jnp.concatenate([value, jnp.zeros((value.shape[0], extra), jnp.float32)], axis=1)
    if lane0 - a:
        value = pltpu.roll(value, lane0 - a, 1)
    ref[:, a : a + span] += value


def spin(value, shift):
    shift = shift % value.shape[1]
    return pltpu.roll(value, shift, 1) if shift else value


def only(has, value):
    return jnp.where(has, value, jnp.zeros_like(value))


def lane_z(rows):
    lane = lax.broadcasted_iota(jnp.int32, (rows, LW), 1).astype(jnp.float32)
    y = jnp.floor((lane + 0.5) * (1.0 / SZ))
    return lane - SZ * y, y


def make_onehot(base_ref, hot):
    flat = base_ref[1:2, :] * SZ + base_ref[2:3, :]
    flat = jnp.broadcast_to(flat, (16, flat.shape[1])).astype(jnp.int16)
    row = lax.broadcasted_iota(jnp.int32, flat.shape, 0).astype(jnp.int16)
    one, zero = jnp.bfloat16(1), jnp.bfloat16(0)
    for r in range(0, NB, 16):
        hot[r : r + 16, :] = jnp.where(row + jnp.int16(r) == flat, one, zero)


def make_left(terms, base_ref, left):
    count = terms[0].shape[1]
    low = iota((8, count), 0) < 4
    turned = [pltpu.roll(t, 4, 0) for t in terms]
    patterns = []
    for a in range(2):
        def join(p, q):
            return jnp.where(low, turned[p] if a else terms[p], terms[q] if a else turned[q])
        parts = [join(0, 1), join(2, 0), join(1, 2)]
        high = [v.astype(jnp.bfloat16).astype(jnp.float32) for v in parts[:2]]
        high_of_last = parts[2].astype(jnp.bfloat16).astype(jnp.float32)
        groups = [high[0], jnp.where(low, high[1], parts[1] - high[1]), parts[2] - high_of_last]
        patterns.append([
            jnp.concatenate([groups[i], groups[j]], axis=0).astype(jnp.bfloat16) for i, j in ((0, 1), (2, 0), (1, 2))
        ])
    bx = jnp.broadcast_to(base_ref[0:1, :], (16, count))
    step = bx - (iota((16, count), 0) >= 8).astype(jnp.int32)
    bx, step = (v.astype(jnp.float32).astype(jnp.bfloat16) for v in (bx, step))
    zero = jnp.bfloat16(0)
    for t in range(LEFT // 16):
        pair, k = divmod(t, 3)
        x = 2 * pair + (1 if k == 2 else 0)
        where = step if k == 1 else bx
        value = jnp.where(
            where == jnp.bfloat16(x), patterns[0][k],
            jnp.where(where == jnp.bfloat16(x - 1), patterns[1][k], zero))
        left[16 * t : 16 * t + 16, :] = value


def gather_sums(left, hot, sums, acc):
    total = lax.dot_general(left[...], hot[...], (((1,), (1,)), ((), ())), preferred_element_type=jnp.float32)
    for j in range(JB):
        sums[j * LEFT : (j + 1) * LEFT, :] = total[:, j * LANE : (j + 1) * LANE]
    sums[JB * LEFT :, :] = jnp.zeros((8, LANE), jnp.float32)
    row = iota((8, LANE), 0)
    pieces = []
    for bc in range(4):
        tiles = []
        for j in range(JB):
            base = j * LEFT + bc
            column = [
                sums[pl.ds(base + 4 * c, 8, stride=24), :] + sums[pl.ds(base + 12 + 4 * c, 8, stride=24), :]
                for c in range(3)
            ]
            first = sums[pl.ds(base + 192, 8, stride=4), :]
            second = sums[pl.ds(base + 216, 8, stride=4), :]
            first = first + pltpu.roll(first, 5, 0)
            second = pltpu.roll(second + pltpu.roll(second, 5, 0), 4, 0)
            last = jnp.where(row < 3, first, jnp.where((row >= 4) & (row < 7), second, 0.0))
            tiles.append(jnp.concatenate(column + [last], axis=0))
        pieces.append(jnp.concatenate(tiles, axis=1))
    near = [pieces[2 * b] + pltpu.roll(pieces[2 * b + 1], 1, 1) for b in range(2)]
    total = near[0] + pltpu.roll(near[1], SZ, 1)
    total = jnp.concatenate([total, jnp.zeros((ROWS, LW - NB), jnp.float32)], axis=1)
    acc[...] = pltpu.roll(total, OFF, 1)


def damage_terms(part, weight):
    w = weight[...]
    share = part[0:1, :] * w
    return [share, share * part[23:24, :], share * part[24:25, :]]


def velocity_terms(part, weight, slope):
    mass = part[0:1, :]
    scale = -time_step * part[1:2, :]
    terms = []
    for i in range(3):
        term = (mass * part[2 + i : 3 + i, :]) * weight[...]
        for j in range(3):
            term = term + (scale * part[14 + 3 * i + j : 15 + 3 * i + j, :]) * slope[8 * j : 8 * j + 8, :]
        terms.append(term)
    return terms


def send_spots(kind):
    if kind:
        return ((H - 1) * SZ, (H - 1 + CY) * SZ), (H - 1, H - 1 + CZ)
    return ((H - 1) * SZ, CY * SZ), (H - 1, CZ)


def land_spots(kind):
    if kind:
        return ((H - 1) * SZ, (H - 1 + CY) * SZ), (H - 1, H - 1 + CZ)
    return (0, (SY - KEEP) * SZ), (0, SZ - KEEP)


def pack_y(kind, acc, ysend):
    for d, lane0 in enumerate(send_spots(kind)[0]):
        ysend[d] = take(acc[...], lane0, WIDE[kind] * SZ)


def pack_z(kind, acc, zsend, esend):
    wide = WIDE[kind]
    y_at, z_at = send_spots(kind)
    z, _ = lane_z(8)
    for d, z0 in enumerate(z_at):
        out = jnp.zeros((8, LW), jnp.float32)
        for s in range(4):
            value = spin(acc[8 * s : 8 * s + 8, :], s * wide - z0)
            out = jnp.where((z >= s * wide) & (z < (s + 1) * wide), value, out)
        zsend[d] = out[:, ZA:ZB]
        for e, lane0 in enumerate(y_at):
            esend[2 * e + d] = take(out, lane0, wide * SZ)


def land_y(kind, acc, yrecv, has):
    for d, lane0 in enumerate(land_spots(kind)[0]):
        put_add(acc, lane0, WIDE[kind] * SZ, only(has(2 * d - 1, 0), yrecv[d]))


def land_z(kind, acc, zrecv, erecv, zin, has):
    wide = WIDE[kind]
    y_at, z_at = land_spots(kind)
    z, _ = lane_z(8)
    for d, z0 in enumerate(z_at):
        zin[:, :ZA] = jnp.zeros((8, ZA), jnp.float32)
        zin[:, ZB:] = jnp.zeros((8, LW - ZB), jnp.float32)
        zin[:, ZA:ZB] = only(has(0, 2 * d - 1), zrecv[d])
        for e, lane0 in enumerate(y_at):
            put_add(zin, lane0, wide * SZ, only(has(2 * e - 1, 2 * d - 1), erecv[2 * e + d]))
        whole = zin[...]
        for s in range(4):
            value = jnp.where((z >= s * wide) & (z < (s + 1) * wide), whole, 0.0)
            acc[8 * s : 8 * s + 8, :] += spin(value, z0 - s * wide)


def tail_rows(last, c):
    row = iota(last.shape, 0)
    first = spin0(last, -c)
    second = spin0(last, -c - 3)
    return jnp.where(row == 0, first, jnp.where(row == 1, second, 0.0))


def spin0(value, shift):
    shift = shift % value.shape[0]
    return pltpu.roll(value, shift, 0) if shift else value


def build_full(acc, low, high, has_low, has_high):
    row = iota((8, LW), 0)
    own_last, low_last = acc[24:32, :], low[24:32, :]
    out = []
    for c in range(3):
        at = slice(8 * c, 8 * c + 8)
        first = only(has_low, jnp.where(row >= 4, low[at, :], 0.0))
        middle = acc[at, :] + only(has_low, tail_rows(low_last, c))
        last = tail_rows(own_last, c) + only(has_high, jnp.where(row < 6, high[at, :], 0.0))
        out.append(jnp.concatenate([first, middle, last], axis=0))
    return out


def relax_all(place, nodes, full, damage_out):
    ix, iy, iz = place
    z, y = lane_z(1)
    gz = z - H + (iz * CZ).astype(jnp.float32)
    gy = y - H + (iy * CY).astype(jnp.float32)
    flat_in = (gz >= 0) & (gz < nodes[2]) & (gy >= 0) & (gy < nodes[1]) & (y < SY)
    row = lax.broadcasted_iota(jnp.int32, (RD, 1), 0)
    gx = row - 4 - H + ix * CX
    row_in = (gx >= 0) & (gx < nodes[0]) & (row >= 4) & (row < 4 + SX)
    inside = row_in.astype(jnp.float32) * flat_in.astype(jnp.float32)
    mass = jnp.maximum(full[0], mass_floor)
    factor = inside / mass
    damage = full[1] * factor
    drive = full[2] * factor
    keep = (1.0 - relax_rate * (6.0 * length_sq + 1.0)) * inside - (2.0 * relax_rate) * drive
    push = (2.0 * relax_rate) * drive
    spread = (relax_rate * length_sq) * inside
    for _ in range(SUBSTEPS):
        ring = (
            pltpu.roll(damage, 1, 0)
            + pltpu.roll(damage, RD - 1, 0)
            + pltpu.roll(damage, SZ, 1)
            + pltpu.roll(damage, LW - SZ, 1)
            + pltpu.roll(damage, 1, 1)
            + pltpu.roll(damage, LW - 1, 1)
        )
        damage = spread * ring + keep * damage + push
    own = pltpu.roll(damage, RD - 4 - H, 0)[0:CX]
    for y in range(CY):
        damage_out[:, y, :] = pltpu.roll(own, LW - (H + y) * SZ - H, 1)[:, :CZ]
    return damage, factor


def make_fields(damage, factor, acc, low, high, has_low, has_high, field_left, lhs):
    row = iota((8, LW), 0)
    last = acc[24:32, :]
    low_last = only(has_low, low[24:32, :])
    velocity = []
    for c in range(3):
        at = slice(8 * c, 8 * c + 8)
        first = acc[at, :] + tail_rows(low_last, c)
        velocity.append(first * factor[8:16])
        from_high = only(has_high, high[at, :])
        last = last + jnp.where(row == c, spin0(from_high, c), jnp.where(row == 4 + c, spin0(from_high, 3 + c), 0.0))
    pair = lambda v: jnp.where(row < 4, jnp.broadcast_to(v[16:17], row.shape), jnp.broadcast_to(v[17:18], row.shape))
    last = jnp.where((row == 3) | (row == 7), pair(damage), last * pair(factor))
    whole = jnp.concatenate(velocity + [damage[8:16], last], axis=0)
    whole = pltpu.roll(whole, LW - OFF, 1)[:, :NB]
    turned = [whole, pltpu.roll(whole, NB - 1, 1)]
    for bc in range(4):
        moved = turned[bc & 1]
        if bc >> 1:
            moved = pltpu.roll(moved, NB - SZ, 1)
        for j in range(JB):
            lanes = slice(j * LANE, (j + 1) * LANE)
            for f in range(4):
                field_left[pl.ds(j * FL + 4 * f + bc, 8, stride=16), :] = moved[8 * f : 8 * f + 8, lanes]
            field_left[pl.ds(j * FL + 128 + bc, 8, stride=4), :] = moved[32:40, lanes]
    for j in range(JB):
        value = field_left[j * FL : (j + 1) * FL, :]
        high_part = value.astype(jnp.bfloat16)
        lhs[:FL, j * LANE : (j + 1) * LANE] = high_part
        lhs[FL:, j * LANE : (j + 1) * LANE] = (value - high_part.astype(jnp.float32)).astype(jnp.bfloat16)


def turn(group, natural, turned, bins):
    for j in range(bins):
        turned[(group * bins + j) * 8 : (group * bins + j + 1) * 8, :] = natural(j)


def corners(half, hot, lhs, got_ref, bx_ref):
    lanes = slice(half * TAIL, (half + 1) * TAIL)
    got = jnp.dot(lhs[...], hot[:, lanes], preferred_element_type=jnp.float32)
    for j in range(MOST):
        got_ref[j * 2 * FL : (j + 1) * 2 * FL, :] = got[:, j * LANE : (j + 1) * LANE]
    bx = bx_ref[MOST * half : MOST * half + MOST, :]
    at = [bx == x for x in range(CX + 1)]
    out = [[None] * 8 for _ in range(4)]
    for f in range(4):
        for bc in range(4):
            near = [jnp.zeros((MOST, LANE), jnp.float32)] * 2
            for x in range(EX):
                r = 16 * x + 4 * f + bc
                value = got_ref[pl.ds(r, MOST, stride=2 * FL), :] + got_ref[pl.ds(FL + r, MOST, stride=2 * FL), :]
                if x < EX - 1:
                    near[0] = jnp.where(at[x], value, near[0])
                if x > 0:
                    near[1] = jnp.where(at[x - 1], value, near[1])
            out[f][bc], out[f][4 + bc] = near
    return out


def total(values):
    while len(values) > 1:
        values = [a + b for a, b in zip(values[::2], values[1::2])]
    return values[0]


def move(corner, w, g, p):
    moved = [total([w(k) * corner[i][k] for k in range(8)]) for i in range(3)]
    velgrad = [[total([corner[i][k] * g(j, k) for k in range(8)]) for j in range(3)] for i in range(3)]
    damaged = jnp.maximum(p(23), total([w(k) * corner[3][k] for k in range(8)]))
    deform = [[p(5 + 3 * i + j) for j in range(3)] for i in range(3)]
    stretch = [[(1.0 if i == j else 0.0) + time_step * velgrad[i][j] for j in range(3)] for i in range(3)]
    mapped = [
        stretch[i][0] * deform[0][j] + stretch[i][1] * deform[1][j] + stretch[i][2] * deform[2][j]
        for i in range(3) for j in range(3)
    ]
    return moved + mapped + [damaged]


def finish(late, early):
    moved, m, damaged = late[:3], late[3:12], late[12]
    mapped = [m[0:3], m[3:6], m[6:9]]
    jacobian = (
        mapped[0][0] * (mapped[1][1] * mapped[2][2] - mapped[1][2] * mapped[2][1])
        - mapped[0][1] * (mapped[1][0] * mapped[2][2] - mapped[1][2] * mapped[2][0])
        + mapped[0][2] * (mapped[1][0] * mapped[2][1] - mapped[1][1] * mapped[2][0])
    )
    left = {}
    for i in range(3):
        for j in range(i, 3):
            left[i, j] = mapped[i][0] * mapped[j][0] + mapped[i][1] * mapped[j][1] + mapped[i][2] * mapped[j][2]
            left[j, i] = left[i, j]
    degrade = (1.0 - damaged) ** 2
    swell = bulk_coef * (jacobian - 1.0)
    stress = []
    for i in range(3):
        for j in range(3):
            term = shear_mod * (left[i, j] - (1.0 if i == j else 0.0))
            if i == j:
                term = term + swell
            stress.append(degrade * term)
    energy = 0.5 * shear_mod * (left[0, 0] + left[1, 1] + left[2, 2] - 3.0) + 0.5 * bulk_coef * (jacobian - 1.0) ** 2
    history = jnp.maximum(early[2], energy)
    position = [early[3 + i] + time_step * moved[i] for i in range(3)]
    return early[:2] + moved + m + stress + [damaged, history] + position


def step_kernel(
    sizes, part, base_ref, weight, slope, counts, out, prior_out, damage_out,
    hot, left, sums, acc_d, acc_v, zin, field_left, lhs, got, turned, bx_ref,
    ysend_d, yrecv_d, zsend_d, zrecv_d, esend_d, erecv_d, ysend_v, yrecv_v, zsend_v, zrecv_v, esend_v, erecv_v,
    xrecv_d, xrecv_v, early_send, early_recv, late_send, late_recv, send_sem, recv_sem,
):
    names = ("gx", "gy", "gz")
    place = [lax.axis_index(a) for a in names]
    has_low = [i > 0 for i in place]
    has_high = [i < n - 1 for i, n in zip(place, sizes)]
    last = sizes[2]
    following, previous = lax.rem(place[2] + 1, last), lax.rem(place[2] + last - 1, last)
    count = part.shape[1]
    bins = count // BIN

    def has(dy, dz):
        found = None
        for k, d in ((1, dy), (2, dz)):
            if d:
                one = has_high[k] if d > 0 else has_low[k]
                found = one if found is None else found & one
        return found

    def device(dy, dz):
        return {names[k]: place[k] + d for k, d in ((1, dy), (2, dz)) if d}

    barrier = pltpu.get_barrier_semaphore()
    waits = 2
    ahead = [(has_low[0], {"gx": place[0] - 1}), (has_high[0], {"gx": place[0] + 1})]
    for exists, other in ahead + [(has(*d), device(*d)) for d in DIRS]:
        @pl.when(exists)
        def _(other=other):
            pl.semaphore_signal(barrier, inc=1, device_id=other, device_id_type=MESH)
        waits = waits + exists.astype(jnp.int32)
    for other in (following, previous):
        pl.semaphore_signal(barrier, inc=1, device_id={"gz": other}, device_id_type=MESH)

    pending = []

    def copy_to(slot, back, src, dst, other):
        return pltpu.make_async_remote_copy(
            src_ref=src, dst_ref=dst, send_sem=send_sem.at[slot], recv_sem=recv_sem.at[back],
            device_id=other, device_id_type=MESH)

    def bufs(kind):
        if kind:
            return (ysend_v, yrecv_v), (zsend_v, zrecv_v), (esend_v, erecv_v)
        return (ysend_d, yrecv_d), (zsend_d, zrecv_d), (esend_d, erecv_d)

    def message(kind, dy, dz):
        y, z = (dy + 1) // 2, (dz + 1) // 2
        if dz == 0:
            (src, dst), at, back = bufs(kind)[0], y, 1 - y
            base = 0
        elif dy == 0:
            (src, dst), at, back = bufs(kind)[1], z, 1 - z
            base = 2
        else:
            (src, dst), at, back = bufs(kind)[2], 2 * y + z, 2 * (1 - y) + 1 - z
            base = 4
        base += 8 * kind
        return copy_to(base + at, base + back, src.at[at], dst.at[back], device(dy, dz))

    def start(kind, chosen):
        for d in chosen:
            copy = message(kind, *d)
            pending.append((has(*d), copy))
            @pl.when(has(*d))
            def _(copy=copy):
                copy.start()

    def arrive(kind, chosen):
        for dy, dz in chosen:
            copy = message(kind, -dy, -dz)
            @pl.when(has(dy, dz))
            def _(copy=copy):
                copy.wait_recv()

    faces_y = [(-1, 0), (1, 0)]
    others = [d for d in DIRS if d[1] != 0]

    def x_messages(kind):
        acc, recv = (acc_v, xrecv_v) if kind else (acc_d, xrecv_d)
        base = 16 + 2 * kind
        return [copy_to(base + d, base + 1 - d, acc, recv.at[1 - d], {"gx": place[0] + 2 * d - 1}) for d in range(2)]

    def x_start(kind):
        for (exists, _), copy in zip(ahead, x_messages(kind)):
            pending.append((exists, copy))
            @pl.when(exists)
            def _(copy=copy):
                copy.start()

    def x_arrive(kind):
        made = x_messages(kind)
        for exists, copy in ((has_low[0], made[1]), (has_high[0], made[0])):
            @pl.when(exists)
            def _(copy=copy):
                copy.wait_recv()

    def ring(slot, src, dst):
        copy = copy_to(slot, slot, src, dst, {"gz": following})
        copy.start()
        return copy

    make_onehot(base_ref, hot)
    make_left(damage_terms(part, weight), base_ref, left)
    gather_sums(left, hot, sums, acc_d)
    pl.semaphore_wait(barrier, waits)
    pack_y(0, acc_d, ysend_d)
    start(0, faces_y)
    pack_z(0, acc_d, zsend_d, esend_d)
    start(0, others)

    make_left(velocity_terms(part, weight, slope), base_ref, left)
    gather_sums(left, hot, sums, acc_v)
    pack_y(1, acc_v, ysend_v)
    start(1, faces_y)
    pack_z(1, acc_v, zsend_v, esend_v)
    start(1, others)

    lanes = lambda j: slice(j * LANE, (j + 1) * LANE)
    for j in range(bins):
        for group in range(3):
            turned[(group * bins + j) * 8 : (group * bins + j + 1) * 8, :] = part[8 * group : 8 * group + 8, lanes(j)]
        turned[(3 * bins + j) * 8 : (3 * bins + j) * 8 + 4, :] = part[24:28, lanes(j)]
        turned[(4 * bins + j) * 8 : (4 * bins + j + 1) * 8, :] = weight[:, lanes(j)]
        for group in range(3):
            at = ((5 + group) * bins + j) * 8
            turned[at : at + 8, :] = slope[8 * group : 8 * group + 8, lanes(j)]
        bx_ref[j : j + 1, :] = base_ref[0:1, lanes(j)]

    def dense(half):
        def read(group, s):
            return turned[pl.ds((group * bins + half * MOST) * 8 + s, MOST, stride=8), :]
        return (
            lambda k: read(4, k), lambda j, k: read(5 + j, k), lambda r: read(r // 8, r % 8)
        )

    halves = bins // MOST
    flying = []
    _, _, p = dense(halves - 1)
    early = [p(0), p(1), p(24), p(25), p(26), p(27)]
    early.append(jnp.broadcast_to(counts[0], (8, LANE)).astype(jnp.float32))
    for q, value in enumerate(early):
        early_send[8 * q : 8 * q + 8, :] = value
    flying.append(ring(20, early_send, early_recv))
    for j in range(MOST + bins, 2 * MOST + bins):
        out[j * SLOT : (j + 1) * SLOT, :] = jnp.zeros((SLOT, LANE), jnp.float32)

    arrive(0, faces_y)
    land_y(0, acc_d, yrecv_d, has)
    arrive(0, others)
    land_z(0, acc_d, zrecv_d, erecv_d, zin, has)
    x_start(0)
    arrive(1, faces_y)
    land_y(1, acc_v, yrecv_v, has)
    arrive(1, others)
    land_z(1, acc_v, zrecv_v, erecv_v, zin, has)
    x_start(1)
    x_arrive(0)
    full = build_full(acc_d, xrecv_d.at[0], xrecv_d.at[1], has_low[0], has_high[0])
    nodes = [n * c for n, c in zip(sizes, (CX, CY, CZ))]
    damage, factor = relax_all(place, nodes, full, damage_out)
    x_arrive(1)
    make_fields(damage, factor, acc_v, xrecv_v.at[0], xrecv_v.at[1], has_low[0], has_high[0], field_left, lhs)

    def store(first, values, gone=None):
        for r, value in enumerate(values):
            if gone is not None:
                value = jnp.where(gone, 0.0, value)
            out[pl.ds(first * SLOT + r, MOST, stride=SLOT), :] = value

    for half in reversed(range(halves)):
        w, g, p = dense(half)
        late = move(corners(half, hot, lhs, got, bx_ref), w, g, p)
        gone = None
        if half == halves - 1:
            for q, value in enumerate(late):
                late_send[8 * q : 8 * q + 8, :] = value
            flying.append(ring(21, late_send, late_recv))
            gone = iota((MOST, LANE), 0) + jnp.broadcast_to(counts[0], (MOST, LANE)) >= MOST
        store((half + 1) * MOST, finish(late, [p(0), p(1), p(24), p(25), p(26), p(27)]), gone)

    for copy in flying:
        copy.wait_recv()
    rows = lambda ref, q: ref[8 * q : 8 * q + 8, :]
    store(0, finish([rows(late_recv, q) for q in range(LATE)], [rows(early_recv, q) for q in range(6)]))
    prior_out[...] = rows(early_recv, 6).astype(jnp.int32)
    for copy in flying:
        copy.wait_send()
    for exists, copy in pending:
        @pl.when(exists)
        def _(copy=copy):
            copy.wait_send()


def place_kernel(ext, prior_ref, damage_in, migrated, damage_out, sem, damage_sem):
    start = MOST - prior_ref[0, 0]
    copies = [pltpu.make_async_copy(damage_in, damage_out, damage_sem)]
    for j in range(migrated.shape[1] // BIN):
        copies.append(pltpu.make_async_copy(
            ext.at[pl.ds(pl.multiple_of((start + j) * SLOT, SLOT), PARTS)],
            migrated.at[:, pl.ds(j * BIN, BIN)], sem.at[j]))
    for copy in copies:
        copy.start()
    for copy in copies:
        copy.wait()


def per_device(particles, stencil_base, weights, gradients, counts):
    count = particles.shape[1]
    bins = count // BIN
    sizes = tuple(lax.axis_size(a) for a in ("gx", "gy", "gz"))
    vmem = pl.BlockSpec(memory_space=pltpu.VMEM)
    anywhere = pl.BlockSpec(memory_space=pl.ANY)
    f32 = jnp.float32
    two = lambda *shape: [pltpu.VMEM(shape, f32)] * 2
    ext, prior, near_damage = pl.pallas_call(
        functools.partial(step_kernel, sizes),
        name="step",
        out_shape=(
            pltpu.VMEM(((bins + 2 * MOST) * SLOT, LANE), f32),
            pltpu.VMEM((8, LANE), jnp.int32),
            pltpu.VMEM((CX, CY, CZ), f32),
        ),
        in_specs=[vmem] * 4 + [pl.BlockSpec(memory_space=pltpu.SMEM)],
        out_specs=(vmem,) * 3,
        scratch_shapes=[
            pltpu.VMEM((NB, count), jnp.bfloat16),
            pltpu.VMEM((LEFT, count), jnp.bfloat16),
            pltpu.VMEM((JB * LEFT + 8, LANE), f32),
            pltpu.VMEM((ROWS, LW), f32),
            pltpu.VMEM((ROWS, LW), f32),
            pltpu.VMEM((8, LW), f32),
            pltpu.VMEM((JB * FL, LANE), f32),
            pltpu.VMEM((2 * FL, NB), jnp.bfloat16),
            pltpu.VMEM((MOST * 2 * FL, LANE), f32),
            pltpu.VMEM((GROUPS * bins * 8, LANE), f32),
            pltpu.VMEM((bins, LANE), jnp.int32),
            *two(2, ROWS, FACE[0]),
            *two(2, 8, ZB - ZA),
            *two(4, 8, FACE[0]),
            *two(2, ROWS, FACE[1]),
            *two(2, 8, ZB - ZA),
            *two(4, 8, FACE[1]),
            *two(2, ROWS, LW),
            *two(EARLY * 8, LANE),
            *two(LATE * 8, LANE),
            pltpu.SemaphoreType.DMA((22,)),
            pltpu.SemaphoreType.DMA((22,)),
        ],
        compiler_params=pltpu.CompilerParams(
            collective_id=0, has_side_effects=True, vmem_limit_bytes=60 * 1024 * 1024
        ),
    )(particles, stencil_base, weights, gradients.reshape(24, count), counts)
    return pl.pallas_call(
        place_kernel,
        name="place",
        out_shape=(
            jax.ShapeDtypeStruct((PARTS, count + TAIL), f32),
            jax.ShapeDtypeStruct((CX, CY, CZ), f32),
        ),
        in_specs=[anywhere, vmem, anywhere],
        out_specs=(anywhere,) * 2,
        scratch_shapes=[pltpu.SemaphoreType.DMA((bins + MOST,)), pltpu.SemaphoreType.DMA(())],
        compiler_params=pltpu.CompilerParams(vmem_limit_bytes=4 * 1024 * 1024),
    )(ext, prior, near_damage)


def solution(mesh):
    return jax.shard_map(
        per_device,
        mesh=mesh,
        in_specs=(
            P(None, ("gx", "gy", "gz")),
            P(None, ("gx", "gy", "gz")),
            P(None, ("gx", "gy", "gz")),
            P(None, None, ("gx", "gy", "gz")),
            P(("gx", "gy", "gz")),
        ),
        out_specs=(P(None, ("gx", "gy", "gz")), P("gx", "gy", "gz")),
        check_vma=False,
    )
```

time: 25.4 us -> 21.3 us (0.84)
  Pallas kernels: 23.9 us -> 19.8 us
    pallas_call x1, Pallas kernels: 23.1 us -> 18.7 us  [per_device(): pl.pallas_call(functools.partial(step_kernel, sizes), name='step', out_sh...]
    pallas_call x1, Pallas kernels: 0.81 us -> 1.1 us  [per_device(): pl.pallas_call(place_kernel, name='place', out_shape=(jax.ShapeDtypeStruc...]
where the time goes in v2:
time: 21.3 us; the launch traced here: 21.1 us
  Pallas kernels  19.8 us (93%)
  between operations  1.29 us (6%)
    pallas_call x1, Pallas kernels, per_device(): pl.pallas_call(functools.partial(step_kernel, sizes), name='step', out_sh...  18.7 us
    pallas_call x1, Pallas kernels, per_device(): pl.pallas_call(place_kernel, name='place', out_shape=(jax.ShapeDtypeStruc...  1.1 us

profile of v2, /device:TPU:0, one launch (start us, length us, event | category | flops | bytes accessed | tf_op | source)
XLA Modules:
  0.0 21.1 jit_solution(2925345366099579356)
XLA Ops:
  1.3 18.7 %step.1 = (f32[1024,128]{1,0:T(8,128)S(1)}, s32[8,128]{1,0:T(8,128)S(1)}, f32[8,16,32]{2,1,0:T(8,128)S(1)}) custom-call(f32[28,2048]{1,0:T(8,128)} %part.1, s32[3,2048]{1,0:T(4,128)} %base_ref.1, f32[8,2048]{1,0:T(8,128)} %weight.1, f32[24,2048]{1,0:T(8,128)} %bitcast.1, s32[1]{0:T(128)S(6)} %copy.7.counts), custom_call_target="tpu_custom_call" | custom-call | tf_op jit(solution)/shard_map/step/pallas_call | solution.py:616
  20.0 1.1 %place.1 = (f32[28,3072]{1,0:T(8,128)}, f32[8,16,32]{2,1,0:T(8,128)}) custom-call(f32[1024,128]{1,0:T(8,128)S(1)} %get-tuple-element.5.ext, s32[8,128]{1,0:T(8,128)S(1)} %get-tuple-element.6.prior_ref, f32[8,16,32]{2,1,0:T(8,128)S(1)} %get-tuple-element.7.damage_in), custom_call_target="tpu_custom_call" | custom-call | tf_op jit(solution)/shard_map/place/pallas_call | solution.py:654

commit v3 on v2

--- a/solution.py
+++ b/solution.py
@@ -32,8 +32,9 @@
 EX, EY, EZ = CX + 2, CY + 2, CZ + 2
 SX, SY, SZ = CX + 2 * H, CY + 2 * H, CZ + 2 * H
 LANE = 128
+MX = 256
 LW = up_to(SY * SZ, LANE)
-NB = up_to((CY + 1) * SZ + CZ + 2, LANE)
+NB = up_to((CY + 1) * SZ + CZ + 2, MX)
 JB = NB // LANE
 OFF = (H - 1) * SZ + H - 1
 KEEP = H + 1
@@ -95,16 +96,15 @@
     return lane - SZ * y, y
 
 
-def make_onehot(base_ref, hot):
-    flat = base_ref[1:2, :] * SZ + base_ref[2:3, :]
-    flat = jnp.broadcast_to(flat, (16, flat.shape[1])).astype(jnp.int16)
-    row = lax.broadcasted_iota(jnp.int32, flat.shape, 0).astype(jnp.int16)
+def onehot(base, first):
+    shape = (16, base.shape[1])
+    flat = jnp.broadcast_to(base[1:2, :] * SZ + base[2:3, :], shape) - iota(shape, 0)
+    flat = flat.astype(jnp.int16)
     one, zero = jnp.bfloat16(1), jnp.bfloat16(0)
-    for r in range(0, NB, 16):
-        hot[r : r + 16, :] = jnp.where(row + jnp.int16(r) == flat, one, zero)
-
-
-def make_left(terms, base_ref, left):
+    return jnp.concatenate([jnp.where(flat == jnp.int16(first + r), one, zero) for r in range(0, MX, 16)], axis=0)
+
+
+def make_left(terms, base):
     count = terms[0].shape[1]
     low = iota((8, count), 0) < 4
     turned = [pltpu.roll(t, 4, 0) for t in terms]
@@ -119,10 +119,11 @@
         patterns.append([
             jnp.concatenate([groups[i], groups[j]], axis=0).astype(jnp.bfloat16) for i, j in ((0, 1), (2, 0), (1, 2))
         ])
-    bx = jnp.broadcast_to(base_ref[0:1, :], (16, count))
+    bx = jnp.broadcast_to(base[0:1, :], (16, count))
     step = bx - (iota((16, count), 0) >= 8).astype(jnp.int32)
     bx, step = (v.astype(jnp.float32).astype(jnp.bfloat16) for v in (bx, step))
     zero = jnp.bfloat16(0)
+    rows = []
     for t in range(LEFT // 16):
         pair, k = divmod(t, 3)
         x = 2 * pair + (1 if k == 2 else 0)
@@ -130,13 +131,33 @@
         value = jnp.where(
             where == jnp.bfloat16(x), patterns[0][k],
             jnp.where(where == jnp.bfloat16(x - 1), patterns[1][k], zero))
-        left[16 * t : 16 * t + 16, :] = value
-
-
-def gather_sums(left, hot, sums, acc):
-    total = lax.dot_general(left[...], hot[...], (((1,), (1,)), ((), ())), preferred_element_type=jnp.float32)
-    for j in range(JB):
-        sums[j * LEFT : (j + 1) * LEFT, :] = total[:, j * LANE : (j + 1) * LANE]
+        rows.append(value)
+    return jnp.concatenate(rows, axis=0)
+
+
+def scatter(terms, base_ref, sums, acc):
+    count = base_ref.shape[1]
+    tiles = NB // MX
+
+    def multiply(*accs):
+        for k in range(count // MX):
+            lanes = slice(k * MX, (k + 1) * MX)
+            base = base_ref[:, lanes]
+            left = make_left(terms(lanes), base)
+            for n in range(tiles):
+                extra = n == tiles - 1 and tiles % 2
+                m = k % 2 if extra else n % 2
+                pltpu.matmul_push_rhs(onehot(base, n * MX), int(n >= 2), m, transpose=True)
+                pltpu.matmul_acc_lhs(accs[n + m if extra else n], left, load_staged_rhs=int(n >= 2))
+        for n in range(tiles):
+            value = pltpu.matmul_pop(accs[n])
+            if n == tiles - 1 and tiles % 2:
+                value = value + pltpu.matmul_pop(accs[n + 1])
+            for j in range(MX // LANE):
+                at = (n * MX // LANE + j) * LEFT
+                sums[at : at + LEFT, :] = value[:, j * LANE : (j + 1) * LANE]
+
+    pl.run_scoped(multiply, *[pltpu.ACC(n % 2)((LEFT, MX), jnp.float32) for n in range(up_to(tiles, 2))])
     sums[JB * LEFT :, :] = jnp.zeros((8, LANE), jnp.float32)
     row = iota((8, LANE), 0)
     pieces = []
@@ -162,20 +183,24 @@
 
 
 def damage_terms(part, weight):
-    w = weight[...]
-    share = part[0:1, :] * w
-    return [share, share * part[23:24, :], share * part[24:25, :]]
+    def terms(lanes):
+        share = part[0:1, lanes] * weight[:, lanes]
+        return [share, share * part[23:24, lanes], share * part[24:25, lanes]]
+    return terms
 
 
 def velocity_terms(part, weight, slope):
-    mass = part[0:1, :]
-    scale = -time_step * part[1:2, :]
-    terms = []
-    for i in range(3):
-        term = (mass * part[2 + i : 3 + i, :]) * weight[...]
-        for j in range(3):
-            term = term + (scale * part[14 + 3 * i + j : 15 + 3 * i + j, :]) * slope[8 * j : 8 * j + 8, :]
-        terms.append(term)
+    def terms(lanes):
+        mass = part[0:1, lanes]
+        scale = -time_step * part[1:2, lanes]
+        out = []
+        for i in range(3):
+            term = (mass * part[2 + i : 3 + i, lanes]) * weight[:, lanes]
+            for j in range(3):
+                row = 14 + 3 * i + j
+                term = term + (scale * part[row : row + 1, lanes]) * slope[8 * j : 8 * j + 8, lanes]
+            out.append(term)
+        return out
     return terms
 
 
@@ -274,13 +299,12 @@
     push = (2.0 * relax_rate) * drive
     spread = (relax_rate * length_sq) * inside
     for _ in range(SUBSTEPS):
+        pair = damage + pltpu.roll(damage, SZ + 1, 1)
         ring = (
             pltpu.roll(damage, 1, 0)
             + pltpu.roll(damage, RD - 1, 0)
-            + pltpu.roll(damage, SZ, 1)
-            + pltpu.roll(damage, LW - SZ, 1)
-            + pltpu.roll(damage, 1, 1)
-            + pltpu.roll(damage, LW - 1, 1)
+            + pltpu.roll(pair, LW - SZ, 1)
+            + pltpu.roll(pair, LW - 1, 1)
         )
         damage = spread * ring + keep * damage + push
     own = pltpu.roll(damage, RD - 4 - H, 0)[0:CX]
@@ -289,7 +313,7 @@
     return damage, factor
 
 
-def make_fields(damage, factor, acc, low, high, has_low, has_high, field_left, lhs):
+def make_fields(damage, factor, acc, low, high, has_low, has_high, field_left):
     row = iota((8, LW), 0)
     last = acc[24:32, :]
     low_last = only(has_low, low[24:32, :])
@@ -314,23 +338,31 @@
             for f in range(4):
                 field_left[pl.ds(j * FL + 4 * f + bc, 8, stride=16), :] = moved[8 * f : 8 * f + 8, lanes]
             field_left[pl.ds(j * FL + 128 + bc, 8, stride=4), :] = moved[32:40, lanes]
-    for j in range(JB):
-        value = field_left[j * FL : (j + 1) * FL, :]
-        high_part = value.astype(jnp.bfloat16)
-        lhs[:FL, j * LANE : (j + 1) * LANE] = high_part
-        lhs[FL:, j * LANE : (j + 1) * LANE] = (value - high_part.astype(jnp.float32)).astype(jnp.bfloat16)
-
-
-def turn(group, natural, turned, bins):
-    for j in range(bins):
-        turned[(group * bins + j) * 8 : (group * bins + j + 1) * 8, :] = natural(j)
-
-
-def corners(half, hot, lhs, got_ref, bx_ref):
-    lanes = slice(half * TAIL, (half + 1) * TAIL)
-    got = jnp.dot(lhs[...], hot[:, lanes], preferred_element_type=jnp.float32)
-    for j in range(MOST):
-        got_ref[j * 2 * FL : (j + 1) * 2 * FL, :] = got[:, j * LANE : (j + 1) * LANE]
+
+
+def corners(half, base_ref, field_left, got_ref, bx_ref):
+    depth = NB // MX
+    tiles = TAIL // MX
+
+    def multiply(*accs):
+        for k in range(depth):
+            value = jnp.concatenate(
+                [field_left[j * FL : (j + 1) * FL, :] for j in range(k * MX // LANE, (k + 1) * MX // LANE)], axis=1)
+            high = value.astype(jnp.bfloat16)
+            low = (value - high.astype(jnp.float32)).astype(jnp.bfloat16)
+            lhs = jnp.concatenate([high, low], axis=0)
+            for n in range(tiles):
+                at = half * TAIL + n * MX
+                pltpu.matmul_push_rhs(onehot(base_ref[:, at : at + MX], k * MX), n // 2 % 2, n % 2)
+                pltpu.matmul_acc_lhs(accs[n], lhs, load_staged_rhs=n // 2 % 2)
+        for n in range(tiles):
+            value = pltpu.matmul_pop(accs[n])
+            for j in range(MX // LANE):
+                for r in range(0, 2 * FL, 8):
+                    got_ref[pl.ds(r * MOST + n * MX // LANE + j, 8, stride=MOST), :] = (
+                        value[r : r + 8, j * LANE : (j + 1) * LANE])
+
+    pl.run_scoped(multiply, *[pltpu.ACC(n % 2)((2 * FL, MX), jnp.float32) for n in range(tiles)])
     bx = bx_ref[MOST * half : MOST * half + MOST, :]
     at = [bx == x for x in range(CX + 1)]
     out = [[None] * 8 for _ in range(4)]
@@ -339,7 +371,7 @@
             near = [jnp.zeros((MOST, LANE), jnp.float32)] * 2
             for x in range(EX):
                 r = 16 * x + 4 * f + bc
-                value = got_ref[pl.ds(r, MOST, stride=2 * FL), :] + got_ref[pl.ds(FL + r, MOST, stride=2 * FL), :]
+                value = got_ref[r * MOST : (r + 1) * MOST, :] + got_ref[(FL + r) * MOST : (FL + r + 1) * MOST, :]
                 if x < EX - 1:
                     near[0] = jnp.where(at[x], value, near[0])
                 if x > 0:
@@ -396,12 +428,19 @@
 
 
 def step_kernel(
-    sizes, part, base_ref, weight, slope, counts, out, prior_out, damage_out,
-    hot, left, sums, acc_d, acc_v, zin, field_left, lhs, got, turned, bx_ref,
+    sizes, part_in, base_in, weight_in, slope_in, counts, ext, prior_out, damage_out,
+    part, base_ref, weight, slope, load_sem, out, sums, acc_d, acc_v, zin, field_left, got, turned, bx_ref,
     ysend_d, yrecv_d, zsend_d, zrecv_d, esend_d, erecv_d, ysend_v, yrecv_v, zsend_v, zrecv_v, esend_v, erecv_v,
     xrecv_d, xrecv_v, early_send, early_recv, late_send, late_recv, send_sem, recv_sem,
 ):
     names = ("gx", "gy", "gz")
+    loads = [
+        pltpu.make_async_copy(src, dst, load_sem.at[i])
+        for i, (src, dst) in enumerate(
+            ((base_in, base_ref), (part_in, part), (weight_in, weight), (slope_in, slope)))
+    ]
+    for load in loads:
+        load.start()
     place = [lax.axis_index(a) for a in names]
     has_low = [i > 0 for i in place]
     has_high = [i < n - 1 for i, n in zip(place, sizes)]
@@ -500,17 +539,17 @@
         copy.start()
         return copy
 
-    make_onehot(base_ref, hot)
-    make_left(damage_terms(part, weight), base_ref, left)
-    gather_sums(left, hot, sums, acc_d)
+    for load in loads[:3]:
+        load.wait()
+    scatter(damage_terms(part, weight), base_ref, sums, acc_d)
     pl.semaphore_wait(barrier, waits)
     pack_y(0, acc_d, ysend_d)
     start(0, faces_y)
     pack_z(0, acc_d, zsend_d, esend_d)
     start(0, others)
 
-    make_left(velocity_terms(part, weight, slope), base_ref, left)
-    gather_sums(left, hot, sums, acc_v)
+    loads[3].wait()
+    scatter(velocity_terms(part, weight, slope), base_ref, sums, acc_v)
     pack_y(1, acc_v, ysend_v)
     start(1, faces_y)
     pack_z(1, acc_v, zsend_v, esend_v)
@@ -542,8 +581,7 @@
     for q, value in enumerate(early):
         early_send[8 * q : 8 * q + 8, :] = value
     flying.append(ring(20, early_send, early_recv))
-    for j in range(MOST + bins, 2 * MOST + bins):
-        out[j * SLOT : (j + 1) * SLOT, :] = jnp.zeros((SLOT, LANE), jnp.float32)
+    ext[:, (MOST + bins) * LANE :] = jnp.zeros((PARTS, TAIL), jnp.float32)
 
     arrive(0, faces_y)
     land_y(0, acc_d, yrecv_d, has)
@@ -560,17 +598,23 @@
     nodes = [n * c for n, c in zip(sizes, (CX, CY, CZ))]
     damage, factor = relax_all(place, nodes, full, damage_out)
     x_arrive(1)
-    make_fields(damage, factor, acc_v, xrecv_v.at[0], xrecv_v.at[1], has_low[0], has_high[0], field_left, lhs)
+    make_fields(damage, factor, acc_v, xrecv_v.at[0], xrecv_v.at[1], has_low[0], has_high[0], field_left)
 
     def store(first, values, gone=None):
+
         for r, value in enumerate(values):
             if gone is not None:
                 value = jnp.where(gone, 0.0, value)
             out[pl.ds(first * SLOT + r, MOST, stride=SLOT), :] = value
+        for j in range(first, first + MOST):
+            for group in range(up_to(PARTS, 8) // 8):
+                rows = min(8, PARTS - 8 * group)
+                at = j * SLOT + 8 * group
+                ext[8 * group : 8 * group + rows, lanes(j)] = out[at : at + rows, :]
 
     for half in reversed(range(halves)):
         w, g, p = dense(half)
-        late = move(corners(half, hot, lhs, got, bx_ref), w, g, p)
+        late = move(corners(half, base_ref, field_left, got, bx_ref), w, g, p)
         gone = None
         if half == halves - 1:
             for q, value in enumerate(late):
@@ -592,13 +636,13 @@
             copy.wait_send()
 
 
-def place_kernel(ext, prior_ref, damage_in, migrated, damage_out, sem, damage_sem):
-    start = MOST - prior_ref[0, 0]
-    copies = [pltpu.make_async_copy(damage_in, damage_out, damage_sem)]
-    for j in range(migrated.shape[1] // BIN):
-        copies.append(pltpu.make_async_copy(
-            ext.at[pl.ds(pl.multiple_of((start + j) * SLOT, SLOT), PARTS)],
-            migrated.at[:, pl.ds(j * BIN, BIN)], sem.at[j]))
+def place_kernel(ext, prior_ref, damage_in, migrated, damage_out, sem):
+    width = migrated.shape[1]
+    start = pl.multiple_of((MOST - prior_ref[0, 0]) * BIN, BIN)
+    copies = [
+        pltpu.make_async_copy(damage_in, damage_out, sem.at[0]),
+        pltpu.make_async_copy(ext.at[:, pl.ds(start, width)], migrated, sem.at[1]),
+    ]
     for copy in copies:
         copy.start()
     for copy in copies:
@@ -617,21 +661,24 @@
         functools.partial(step_kernel, sizes),
         name="step",
         out_shape=(
-            pltpu.VMEM(((bins + 2 * MOST) * SLOT, LANE), f32),
+            pltpu.VMEM((PARTS, count + 2 * TAIL), f32),
             pltpu.VMEM((8, LANE), jnp.int32),
             pltpu.VMEM((CX, CY, CZ), f32),
         ),
-        in_specs=[vmem] * 4 + [pl.BlockSpec(memory_space=pltpu.SMEM)],
+        in_specs=[anywhere] * 4 + [pl.BlockSpec(memory_space=pltpu.SMEM)],
         out_specs=(vmem,) * 3,
         scratch_shapes=[
-            pltpu.VMEM((NB, count), jnp.bfloat16),
-            pltpu.VMEM((LEFT, count), jnp.bfloat16),
+            pltpu.VMEM((PARTS, count), f32),
+            pltpu.VMEM((3, count), jnp.int32),
+            pltpu.VMEM((8, count), f32),
+            pltpu.VMEM((24, count), f32),
+            pltpu.SemaphoreType.DMA((4,)),
+            pltpu.VMEM(((bins + MOST) * SLOT, LANE), f32),
             pltpu.VMEM((JB * LEFT + 8, LANE), f32),
             pltpu.VMEM((ROWS, LW), f32),
             pltpu.VMEM((ROWS, LW), f32),
             pltpu.VMEM((8, LW), f32),
             pltpu.VMEM((JB * FL, LANE), f32),
-            pltpu.VMEM((2 * FL, NB), jnp.bfloat16),
             pltpu.VMEM((MOST * 2 * FL, LANE), f32),
             pltpu.VMEM((GROUPS * bins * 8, LANE), f32),
             pltpu.VMEM((bins, LANE), jnp.int32),
@@ -660,7 +707,7 @@
         ),
         in_specs=[anywhere, vmem, anywhere],
         out_specs=(anywhere,) * 2,
-        scratch_shapes=[pltpu.SemaphoreType.DMA((bins + MOST,)), pltpu.SemaphoreType.DMA(())],
+        scratch_shapes=[pltpu.SemaphoreType.DMA((2,))],
         compiler_params=pltpu.CompilerParams(vmem_limit_bytes=4 * 1024 * 1024),
     )(ext, prior, near_damage)
 

time: 21.3 us -> 19 us (0.89)
  Pallas kernels: 19.8 us -> 17.6 us
    pallas_call x1, Pallas kernels: 18.7 us -> 16.8 us  [per_device(): pl.pallas_call(functools.partial(step_kernel, sizes), name='step', out_sh...]
    pallas_call x1, Pallas kernels: 1.1 us -> 0.8 us  [per_device(): pl.pallas_call(place_kernel, name='place', out_shape=(jax.ShapeDtypeStruc...]
where the time goes in v3:
time: 19 us; the launch traced here: 18.8 us
  Pallas kernels  17.6 us (93%)
  between operations  1.29 us (7%)
    pallas_call x1, Pallas kernels, per_device(): pl.pallas_call(functools.partial(step_kernel, sizes), name='step', out_sh...  16.8 us
    pallas_call x1, Pallas kernels, per_device(): pl.pallas_call(place_kernel, name='place', out_shape=(jax.ShapeDtypeStruc...  0.8 us

profile of v3, /device:TPU:0, one launch (start us, length us, event | category | flops | bytes accessed | tf_op | source)
XLA Modules:
  0.0 18.8 jit_solution(4846719401928994428)
XLA Ops:
  1.3 16.8 %step.1 = (f32[28,4096]{1,0:T(8,128)S(1)}, s32[8,128]{1,0:T(8,128)S(1)}, f32[8,16,32]{2,1,0:T(8,128)S(1)}) custom-call(f32[28,2048]{1,0:T(8,128)} %part_in.1, s32[3,2048]{1,0:T(4,128)} %base_in.1, f32[8,2048]{1,0:T(8,128)} %weight_in.1, f32[24,2048]{1,0:T(8,128)} %bitcast.1, s32[1]{0:T(128)S(6)} %copy.7.counts), custom_call_target="tpu_custom_call" | custom-call | tf_op jit(solution)/shard_map/step/pallas_call | solution.py:660
  18.0 0.8 %place.1 = (f32[28,3072]{1,0:T(8,128)}, f32[8,16,32]{2,1,0:T(8,128)}) custom-call(f32[28,4096]{1,0:T(8,128)S(1)} %get-tuple-element.5.ext, s32[8,128]{1,0:T(8,128)S(1)} %get-tuple-element.6.prior_ref, f32[8,16,32]{2,1,0:T(8,128)S(1)} %get-tuple-element.7.damage_in), custom_call_target="tpu_custom_call" | custom-call | tf_op jit(solution)/shard_map/place/pallas_call | solution.py:701

commit v4 on v3

--- a/solution.py
+++ b/solution.py
@@ -40,8 +40,7 @@
 KEEP = H + 1
 RD = 24
 ROWS = 32
-LEFT = EX * 24
-PATTERNS = 3
+LEFT = up_to(EX * 12, 16)
 WIDE = {0: KEEP, 1: 2}
 FACE = {0: up_to(KEEP * SZ, LANE), 1: up_to(2 * SZ, LANE)}
 ZA, ZB = (H - 1) * SZ // LANE * LANE, up_to((H + CY + 1) * SZ, LANE)
@@ -50,8 +49,13 @@
 PARTS = 28
 SLOT = 32
 GROUPS = 8
+CHUNKS = 1
+EARLY_PART = 4
 LATE = 13
 EARLY = 7
+FOLDS = 3
+FY = EY // FOLDS
+ZF = up_to(FY * SZ, LANE)
 DIRS = [(dy, dz) for dy in (-1, 0, 1) for dz in (-1, 0, 1) if (dy, dz) != (0, 0)]
 
 
@@ -104,7 +108,19 @@
     return jnp.concatenate([jnp.where(flat == jnp.int16(first + r), one, zero) for r in range(0, MX, 16)], axis=0)
 
 
-def make_left(terms, base):
+def split(value):
+    high = value.astype(jnp.bfloat16)
+    return high, (value - high.astype(jnp.float32)).astype(jnp.bfloat16)
+
+
+def bin_steps(base):
+    count = base.shape[1]
+    bx = jnp.broadcast_to(base[0:1, :], (16, count))
+    steps = [bx - (iota((16, count), 0) >= cut).astype(jnp.int32) for cut in (12, 8, 4)]
+    return [v.astype(jnp.float32).astype(jnp.bfloat16) for v in steps]
+
+
+def make_left(terms, steps):
     count = terms[0].shape[1]
     low = iota((8, count), 0) < 4
     turned = [pltpu.roll(t, 4, 0) for t in terms]
@@ -113,68 +129,54 @@
         def join(p, q):
             return jnp.where(low, turned[p] if a else terms[p], terms[q] if a else turned[q])
         parts = [join(0, 1), join(2, 0), join(1, 2)]
-        high = [v.astype(jnp.bfloat16).astype(jnp.float32) for v in parts[:2]]
-        high_of_last = parts[2].astype(jnp.bfloat16).astype(jnp.float32)
-        groups = [high[0], jnp.where(low, high[1], parts[1] - high[1]), parts[2] - high_of_last]
-        patterns.append([
-            jnp.concatenate([groups[i], groups[j]], axis=0).astype(jnp.bfloat16) for i, j in ((0, 1), (2, 0), (1, 2))
-        ])
-    bx = jnp.broadcast_to(base[0:1, :], (16, count))
-    step = bx - (iota((16, count), 0) >= 8).astype(jnp.int32)
-    bx, step = (v.astype(jnp.float32).astype(jnp.bfloat16) for v in (bx, step))
+        patterns.append([split(jnp.concatenate([parts[i], parts[j]], axis=0)) for i, j in ((0, 1), (2, 0), (1, 2))])
     zero = jnp.bfloat16(0)
-    rows = []
+    rows = [[], []]
     for t in range(LEFT // 16):
-        pair, k = divmod(t, 3)
-        x = 2 * pair + (1 if k == 2 else 0)
-        where = step if k == 1 else bx
-        value = jnp.where(
-            where == jnp.bfloat16(x), patterns[0][k],
-            jnp.where(where == jnp.bfloat16(x - 1), patterns[1][k], zero))
-        rows.append(value)
-    return jnp.concatenate(rows, axis=0)
-
-
-def scatter(terms, base_ref, sums, acc):
-    count = base_ref.shape[1]
+        k = t % 3
+        x = 16 * t // 12
+        near, far = steps[k] == jnp.bfloat16(x), steps[k] == jnp.bfloat16(x - 1)
+        for part in range(2):
+            rows[part].append(jnp.where(near, patterns[0][k][part], jnp.where(far, patterns[1][k][part], zero)))
+    return [jnp.concatenate(part, axis=0) for part in rows]
+
+
+def scatter_tiles(terms, base_ref, accs, some, arrived=None):
     tiles = NB // MX
-
-    def multiply(*accs):
-        for k in range(count // MX):
-            lanes = slice(k * MX, (k + 1) * MX)
-            base = base_ref[:, lanes]
-            left = make_left(terms(lanes), base)
-            for n in range(tiles):
-                extra = n == tiles - 1 and tiles % 2
-                m = k % 2 if extra else n % 2
-                pltpu.matmul_push_rhs(onehot(base, n * MX), int(n >= 2), m, transpose=True)
-                pltpu.matmul_acc_lhs(accs[n + m if extra else n], left, load_staged_rhs=int(n >= 2))
+    for k in some:
+        if arrived is not None:
+            arrived(k)
+        lanes = slice(k * MX, (k + 1) * MX)
+        base = base_ref[:, lanes]
+        left = make_left(terms(lanes), bin_steps(base))
         for n in range(tiles):
-            value = pltpu.matmul_pop(accs[n])
-            if n == tiles - 1 and tiles % 2:
-                value = value + pltpu.matmul_pop(accs[n + 1])
-            for j in range(MX // LANE):
-                at = (n * MX // LANE + j) * LEFT
-                sums[at : at + LEFT, :] = value[:, j * LANE : (j + 1) * LANE]
-
-    pl.run_scoped(multiply, *[pltpu.ACC(n % 2)((LEFT, MX), jnp.float32) for n in range(up_to(tiles, 2))])
-    sums[JB * LEFT :, :] = jnp.zeros((8, LANE), jnp.float32)
-    row = iota((8, LANE), 0)
+            extra = n == tiles - 1 and tiles % 2
+            m = k % 2 if extra else n % 2
+            acc = accs[n + m if extra else n]
+            pltpu.matmul_push_rhs(onehot(base, n * MX), int(n >= 2), m, transpose=True)
+            pltpu.matmul_acc_lhs(acc, left[0], load_staged_rhs=int(n >= 2))
+            pltpu.matmul_acc_lhs(acc, left[1])
+
+
+def scatter_pop(accs, sums):
+    tiles = NB // MX
+    for n in range(tiles):
+        value = pltpu.matmul_pop(accs[n])
+        if n == tiles - 1 and tiles % 2:
+            value = value + pltpu.matmul_pop(accs[n + 1])
+        for j in range(MX // LANE):
+            at = (n * MX // LANE + j) * LEFT
+            sums[at : at + LEFT, :] = value[:, j * LANE : (j + 1) * LANE]
+
+
+def add_corners(sums, acc):
     pieces = []
     for bc in range(4):
         tiles = []
         for j in range(JB):
             base = j * LEFT + bc
-            column = [
-                sums[pl.ds(base + 4 * c, 8, stride=24), :] + sums[pl.ds(base + 12 + 4 * c, 8, stride=24), :]
-                for c in range(3)
-            ]
-            first = sums[pl.ds(base + 192, 8, stride=4), :]
-            second = sums[pl.ds(base + 216, 8, stride=4), :]
-            first = first + pltpu.roll(first, 5, 0)
-            second = pltpu.roll(second + pltpu.roll(second, 5, 0), 4, 0)
-            last = jnp.where(row < 3, first, jnp.where((row >= 4) & (row < 7), second, 0.0))
-            tiles.append(jnp.concatenate(column + [last], axis=0))
+            column = [sums[pl.ds(base + 4 * c, 8, stride=12), :] for c in range(3)]
+            tiles.append(jnp.concatenate(column + [sums[pl.ds(base + 96, 8, stride=4), :]], axis=0))
         pieces.append(jnp.concatenate(tiles, axis=1))
     near = [pieces[2 * b] + pltpu.roll(pieces[2 * b + 1], 1, 1) for b in range(2)]
     total = near[0] + pltpu.roll(near[1], SZ, 1)
@@ -230,7 +232,10 @@
         for s in range(4):
             value = spin(acc[8 * s : 8 * s + 8, :], s * wide - z0)
             out = jnp.where((z >= s * wide) & (z < (s + 1) * wide), value, out)
-        zsend[d] = out[:, ZA:ZB]
+        if kind:
+            zsend[d] = sum(spin(take(out, (H - 1 + q * FY) * SZ, FY * SZ), 4 * wide * q) for q in range(FOLDS))
+        else:
+            zsend[d] = out[:, ZA:ZB]
         for e, lane0 in enumerate(y_at):
             esend[2 * e + d] = take(out, lane0, wide * SZ)
 
@@ -245,9 +250,18 @@
     y_at, z_at = land_spots(kind)
     z, _ = lane_z(8)
     for d, z0 in enumerate(z_at):
-        zin[:, :ZA] = jnp.zeros((8, ZA), jnp.float32)
-        zin[:, ZB:] = jnp.zeros((8, LW - ZB), jnp.float32)
-        zin[:, ZA:ZB] = only(has(0, 2 * d - 1), zrecv[d])
+        if kind:
+            zin[...] = jnp.zeros((8, LW), jnp.float32)
+            folded = only(has(0, 2 * d - 1), zrecv[d])
+            short, lane = z[:, :ZF], iota((8, ZF), 1)
+            for q in range(FOLDS):
+                z1 = 4 * wide * q
+                mine = (short >= z1) & (short < z1 + 4 * wide) & (lane < FY * SZ)
+                put_add(zin, (H - 1 + q * FY) * SZ, FY * SZ, spin(jnp.where(mine, folded, 0.0), -z1))
+        else:
+            zin[:, :ZA] = jnp.zeros((8, ZA), jnp.float32)
+            zin[:, ZB:] = jnp.zeros((8, LW - ZB), jnp.float32)
+            zin[:, ZA:ZB] = only(has(0, 2 * d - 1), zrecv[d])
         for e, lane0 in enumerate(y_at):
             put_add(zin, lane0, wide * SZ, only(has(2 * e - 1, 2 * d - 1), erecv[2 * e + d]))
         whole = zin[...]
@@ -259,7 +273,7 @@
 def tail_rows(last, c):
     row = iota(last.shape, 0)
     first = spin0(last, -c)
-    second = spin0(last, -c - 3)
+    second = spin0(last, -c - 2)
     return jnp.where(row == 0, first, jnp.where(row == 1, second, 0.0))
 
 
@@ -281,7 +295,7 @@
     return out
 
 
-def relax_all(place, nodes, full, damage_out):
+def relax_all(place, nodes, full, line):
     ix, iy, iz = place
     z, y = lane_z(1)
     gz = z - H + (iz * CZ).astype(jnp.float32)
@@ -298,19 +312,26 @@
     keep = (1.0 - relax_rate * (6.0 * length_sq + 1.0)) * inside - (2.0 * relax_rate) * drive
     push = (2.0 * relax_rate) * drive
     spread = (relax_rate * length_sq) * inside
+    tiles = LW // LANE
+    line[0:8, :] = jnp.zeros((8, LANE), jnp.float32)
+    line[8 + tiles * RD :, :] = jnp.zeros((8, LANE), jnp.float32)
     for _ in range(SUBSTEPS):
+        for j in range(tiles):
+            line[8 + j * RD : 8 + (j + 1) * RD, :] = damage[:, j * LANE : (j + 1) * LANE]
         pair = damage + pltpu.roll(damage, SZ + 1, 1)
-        ring = (
-            pltpu.roll(damage, 1, 0)
-            + pltpu.roll(damage, RD - 1, 0)
-            + pltpu.roll(pair, LW - SZ, 1)
-            + pltpu.roll(pair, LW - 1, 1)
-        )
+        along = jnp.concatenate(
+            [line[pl.ds(7 + j * RD, RD), :] + line[pl.ds(9 + j * RD, RD), :] for j in range(tiles)], axis=1)
+        ring = along + pltpu.roll(pair, LW - SZ, 1) + pltpu.roll(pair, LW - 1, 1)
         damage = spread * ring + keep * damage + push
-    own = pltpu.roll(damage, RD - 4 - H, 0)[0:CX]
+    for j in range(tiles):
+        line[8 + j * RD : 8 + (j + 1) * RD, :] = damage[:, j * LANE : (j + 1) * LANE]
+    return damage, factor
+
+
+def show_damage(line, damage_out):
+    own = jnp.concatenate([line[pl.ds(8 + j * RD + 4 + H, CX), :] for j in range(LW // LANE)], axis=1)
     for y in range(CY):
         damage_out[:, y, :] = pltpu.roll(own, LW - (H + y) * SZ - H, 1)[:, :CZ]
-    return damage, factor
 
 
 def make_fields(damage, factor, acc, low, high, has_low, has_high, field_left):
@@ -323,8 +344,9 @@
         first = acc[at, :] + tail_rows(low_last, c)
         velocity.append(first * factor[8:16])
         from_high = only(has_high, high[at, :])
-        last = last + jnp.where(row == c, spin0(from_high, c), jnp.where(row == 4 + c, spin0(from_high, 3 + c), 0.0))
+        last = last + jnp.where(row == c, spin0(from_high, c), jnp.where(row == 3 + c, spin0(from_high, 2 + c), 0.0))
     pair = lambda v: jnp.where(row < 4, jnp.broadcast_to(v[16:17], row.shape), jnp.broadcast_to(v[17:18], row.shape))
+    last = jnp.where(row < 3, last, pltpu.roll(last, 1, 0))
     last = jnp.where((row == 3) | (row == 7), pair(damage), last * pair(factor))
     whole = jnp.concatenate(velocity + [damage[8:16], last], axis=0)
     whole = pltpu.roll(whole, LW - OFF, 1)[:, :NB]
@@ -348,21 +370,20 @@
         for k in range(depth):
             value = jnp.concatenate(
                 [field_left[j * FL : (j + 1) * FL, :] for j in range(k * MX // LANE, (k + 1) * MX // LANE)], axis=1)
-            high = value.astype(jnp.bfloat16)
-            low = (value - high.astype(jnp.float32)).astype(jnp.bfloat16)
-            lhs = jnp.concatenate([high, low], axis=0)
+            high, low = split(value)
             for n in range(tiles):
                 at = half * TAIL + n * MX
                 pltpu.matmul_push_rhs(onehot(base_ref[:, at : at + MX], k * MX), n // 2 % 2, n % 2)
-                pltpu.matmul_acc_lhs(accs[n], lhs, load_staged_rhs=n // 2 % 2)
+                pltpu.matmul_acc_lhs(accs[n], high, load_staged_rhs=n // 2 % 2)
+                pltpu.matmul_acc_lhs(accs[n], low)
         for n in range(tiles):
             value = pltpu.matmul_pop(accs[n])
             for j in range(MX // LANE):
-                for r in range(0, 2 * FL, 8):
+                for r in range(0, FL, 8):
                     got_ref[pl.ds(r * MOST + n * MX // LANE + j, 8, stride=MOST), :] = (
                         value[r : r + 8, j * LANE : (j + 1) * LANE])
 
-    pl.run_scoped(multiply, *[pltpu.ACC(n % 2)((2 * FL, MX), jnp.float32) for n in range(tiles)])
+    pl.run_scoped(multiply, *[pltpu.ACC(n % 2)((FL, MX), jnp.float32) for n in range(tiles)])
     bx = bx_ref[MOST * half : MOST * half + MOST, :]
     at = [bx == x for x in range(CX + 1)]
     out = [[None] * 8 for _ in range(4)]
@@ -371,7 +392,7 @@
             near = [jnp.zeros((MOST, LANE), jnp.float32)] * 2
             for x in range(EX):
                 r = 16 * x + 4 * f + bc
-                value = got_ref[r * MOST : (r + 1) * MOST, :] + got_ref[(FL + r) * MOST : (FL + r + 1) * MOST, :]
+                value = got_ref[r * MOST : (r + 1) * MOST, :]
                 if x < EX - 1:
                     near[0] = jnp.where(at[x], value, near[0])
                 if x > 0:
@@ -427,26 +448,36 @@
     return early[:2] + moved + m + stress + [damaged, history] + position
 
 
-def step_kernel(
-    sizes, part_in, base_in, weight_in, slope_in, counts, ext, prior_out, damage_out,
-    part, base_ref, weight, slope, load_sem, out, sums, acc_d, acc_v, zin, field_left, got, turned, bx_ref,
+def step_kernel(sizes, *refs):
+    slots = up_to(NB // MX, 2)
+    kinds = [pltpu.ACC(n % 2)((LEFT, MX), jnp.float32) for _ in range(2) for n in range(slots)]
+    pl.run_scoped(lambda *accs: step_body(accs, sizes, *refs), *kinds)
+
+
+def step_body(
+    accs, sizes, part_in, base_in, weight_in, slope_in, counts, ext, prior_out, damage_out,
+    part, base_ref, weight, slope, load_sem, out, sums, acc_d, acc_v, zin, line, field_left, got, turned, bx_ref,
     ysend_d, yrecv_d, zsend_d, zrecv_d, esend_d, erecv_d, ysend_v, yrecv_v, zsend_v, zrecv_v, esend_v, erecv_v,
     xrecv_d, xrecv_v, early_send, early_recv, late_send, late_recv, send_sem, recv_sem,
 ):
     names = ("gx", "gy", "gz")
-    loads = [
-        pltpu.make_async_copy(src, dst, load_sem.at[i])
-        for i, (src, dst) in enumerate(
-            ((base_in, base_ref), (part_in, part), (weight_in, weight), (slope_in, slope)))
-    ]
-    for load in loads:
+    count = part.shape[1]
+    chunk = count // CHUNKS
+    loads = []
+    for c in range(CHUNKS):
+        lanes = pl.ds(c * chunk, chunk)
+        loads.append([
+            pltpu.make_async_copy(src.at[:, lanes], dst.at[:, lanes], load_sem.at[4 * c + i])
+            for i, (src, dst) in enumerate(
+                ((base_in, base_ref), (part_in, part), (weight_in, weight), (slope_in, slope)))
+        ])
+    for load in loads[0]:
         load.start()
     place = [lax.axis_index(a) for a in names]
     has_low = [i > 0 for i in place]
     has_high = [i < n - 1 for i, n in zip(place, sizes)]
     last = sizes[2]
     following, previous = lax.rem(place[2] + 1, last), lax.rem(place[2] + last - 1, last)
-    count = part.shape[1]
     bins = count // BIN
 
     def has(dy, dz):
@@ -539,21 +570,36 @@
         copy.start()
         return copy
 
-    for load in loads[:3]:
-        load.wait()
-    scatter(damage_terms(part, weight), base_ref, sums, acc_d)
+    for group in loads[1:]:
+        for load in group:
+            load.start()
+
+    def arrived(k):
+        if k * MX % chunk == 0:
+            for load in loads[k * MX // chunk]:
+                load.wait()
+
+    slots = up_to(NB // MX, 2)
+    spans = count // MX
+    early_spans = spans * EARLY_PART // 8
+
+    scatter_tiles(damage_terms(part, weight), base_ref, accs[:slots], range(spans), arrived)
+    scatter_pop(accs[:slots], sums.at[0])
+    terms = velocity_terms(part, weight, slope)
+    scatter_tiles(terms, base_ref, accs[slots:], range(early_spans))
+    add_corners(sums.at[0], acc_d)
+    pack_z(0, acc_d, zsend_d, esend_d)
+    pack_y(0, acc_d, ysend_d)
     pl.semaphore_wait(barrier, waits)
-    pack_y(0, acc_d, ysend_d)
+    start(0, others)
     start(0, faces_y)
-    pack_z(0, acc_d, zsend_d, esend_d)
-    start(0, others)
-
-    loads[3].wait()
-    scatter(velocity_terms(part, weight, slope), base_ref, sums, acc_v)
+    scatter_tiles(terms, base_ref, accs[slots:], range(early_spans, spans))
+    scatter_pop(accs[slots:], sums.at[1])
+    add_corners(sums.at[1], acc_v)
+    pack_z(1, acc_v, zsend_v, esend_v)
+    start(1, others)
     pack_y(1, acc_v, ysend_v)
     start(1, faces_y)
-    pack_z(1, acc_v, zsend_v, esend_v)
-    start(1, others)
 
     lanes = lambda j: slice(j * LANE, (j + 1) * LANE)
     for j in range(bins):
@@ -596,7 +642,7 @@
     x_arrive(0)
     full = build_full(acc_d, xrecv_d.at[0], xrecv_d.at[1], has_low[0], has_high[0])
     nodes = [n * c for n, c in zip(sizes, (CX, CY, CZ))]
-    damage, factor = relax_all(place, nodes, full, damage_out)
+    damage, factor = relax_all(place, nodes, full, line)
     x_arrive(1)
     make_fields(damage, factor, acc_v, xrecv_v.at[0], xrecv_v.at[1], has_low[0], has_high[0], field_left)
 
@@ -620,6 +666,7 @@
             for q, value in enumerate(late):
                 late_send[8 * q : 8 * q + 8, :] = value
             flying.append(ring(21, late_send, late_recv))
+            show_damage(line, damage_out)
             gone = iota((MOST, LANE), 0) + jnp.broadcast_to(counts[0], (MOST, LANE)) >= MOST
         store((half + 1) * MOST, finish(late, [p(0), p(1), p(24), p(25), p(26), p(27)]), gone)
 
@@ -672,21 +719,22 @@
             pltpu.VMEM((3, count), jnp.int32),
             pltpu.VMEM((8, count), f32),
             pltpu.VMEM((24, count), f32),
-            pltpu.SemaphoreType.DMA((4,)),
+            pltpu.SemaphoreType.DMA((4 * CHUNKS,)),
             pltpu.VMEM(((bins + MOST) * SLOT, LANE), f32),
-            pltpu.VMEM((JB * LEFT + 8, LANE), f32),
+            pltpu.VMEM((2, JB * LEFT, LANE), f32),
             pltpu.VMEM((ROWS, LW), f32),
             pltpu.VMEM((ROWS, LW), f32),
             pltpu.VMEM((8, LW), f32),
+            pltpu.VMEM((16 + LW // LANE * RD, LANE), f32),
             pltpu.VMEM((JB * FL, LANE), f32),
-            pltpu.VMEM((MOST * 2 * FL, LANE), f32),
+            pltpu.VMEM((MOST * FL, LANE), f32),
             pltpu.VMEM((GROUPS * bins * 8, LANE), f32),
             pltpu.VMEM((bins, LANE), jnp.int32),
             *two(2, ROWS, FACE[0]),
             *two(2, 8, ZB - ZA),
             *two(4, 8, FACE[0]),
             *two(2, ROWS, FACE[1]),
-            *two(2, 8, ZB - ZA),
+            *two(2, 8, ZF),
             *two(4, 8, FACE[1]),
             *two(2, ROWS, LW),
             *two(EARLY * 8, LANE),

time: 19 us -> 18.6 us (0.979)
  Pallas kernels: 17.6 us -> 17.1 us
    pallas_call x1, Pallas kernels: 16.8 us -> 16.3 us  [per_device(): pl.pallas_call(functools.partial(step_kernel, sizes), name='step', out_sh...]
where the time goes in v4:
time: 18.6 us; the launch traced here: 18.4 us
  Pallas kernels  17.1 us (92%)
  between operations  1.29 us (7%)
    pallas_call x1, Pallas kernels, per_device(): pl.pallas_call(functools.partial(step_kernel, sizes), name='step', out_sh...  16.3 us
    pallas_call x1, Pallas kernels, per_device(): pl.pallas_call(place_kernel, name='place', out_shape=(jax.ShapeDtypeStruc...  0.8 us

profile of v4, /device:TPU:0, one launch (start us, length us, event | category | flops | bytes accessed | tf_op | source)
XLA Modules:
  0.0 18.4 jit_solution(17320139495088070277)
XLA Ops:
  1.3 16.3 %step.1 = (f32[28,4096]{1,0:T(8,128)S(1)}, s32[8,128]{1,0:T(8,128)S(1)}, f32[8,16,32]{2,1,0:T(8,128)S(1)}) custom-call(f32[28,2048]{1,0:T(8,128)} %refs_0_.1, s32[3,2048]{1,0:T(4,128)} %refs_1_.1, f32[8,2048]{1,0:T(8,128)} %refs_2_.1, f32[24,2048]{1,0:T(8,128)} %bitcast.1, s32[1]{0:T(128)S(6)} %copy.7.refs_4_), custom_call_target="tpu_custom_call" | custom-call | tf_op jit(solution)/shard_map/step/pallas_call | solution.py:707
  17.6 0.8 %place.1 = (f32[28,3072]{1,0:T(8,128)}, f32[8,16,32]{2,1,0:T(8,128)}) custom-call(f32[28,4096]{1,0:T(8,128)S(1)} %get-tuple-element.5.ext, s32[8,128]{1,0:T(8,128)S(1)} %get-tuple-element.6.prior_ref, f32[8,16,32]{2,1,0:T(8,128)S(1)} %get-tuple-element.7.damage_in), custom_call_target="tpu_custom_call" | custom-call | tf_op jit(solution)/shard_map/place/pallas_call | solution.py:749

commit v5 on v4

--- a/solution.py
+++ b/solution.py
@@ -50,7 +50,7 @@
 SLOT = 32
 GROUPS = 8
 CHUNKS = 1
-EARLY_PART = 4
+EARLY_PART = 8
 LATE = 13
 EARLY = 7
 FOLDS = 3
@@ -280,6 +280,15 @@
 def spin0(value, shift):
     shift = shift % value.shape[0]
     return pltpu.roll(value, shift, 0) if shift else value
+
+
+def pack_edge(acc, edge):
+    row = iota((8, LW), 0)
+    out = jnp.zeros((8, LW), jnp.float32)
+    for c in range(3):
+        value = acc[8 * c : 8 * c + 8, :]
+        out = jnp.where(row == c, spin0(value, c), jnp.where(row == 3 + c, spin0(value, 2 + c), out))
+    edge[...] = out
 
 
 def build_full(acc, low, high, has_low, has_high):
@@ -337,14 +346,13 @@
 def make_fields(damage, factor, acc, low, high, has_low, has_high, field_left):
     row = iota((8, LW), 0)
     last = acc[24:32, :]
-    low_last = only(has_low, low[24:32, :])
+    low_last = only(has_low, low[...])
+    last = last + only(has_high, high[...])
     velocity = []
     for c in range(3):
         at = slice(8 * c, 8 * c + 8)
         first = acc[at, :] + tail_rows(low_last, c)
         velocity.append(first * factor[8:16])
-        from_high = only(has_high, high[at, :])
-        last = last + jnp.where(row == c, spin0(from_high, c), jnp.where(row == 3 + c, spin0(from_high, 2 + c), 0.0))
     pair = lambda v: jnp.where(row < 4, jnp.broadcast_to(v[16:17], row.shape), jnp.broadcast_to(v[17:18], row.shape))
     last = jnp.where(row < 3, last, pltpu.roll(last, 1, 0))
     last = jnp.where((row == 3) | (row == 7), pair(damage), last * pair(factor))
@@ -458,7 +466,7 @@
     accs, sizes, part_in, base_in, weight_in, slope_in, counts, ext, prior_out, damage_out,
     part, base_ref, weight, slope, load_sem, out, sums, acc_d, acc_v, zin, line, field_left, got, turned, bx_ref,
     ysend_d, yrecv_d, zsend_d, zrecv_d, esend_d, erecv_d, ysend_v, yrecv_v, zsend_v, zrecv_v, esend_v, erecv_v,
-    xrecv_d, xrecv_v, early_send, early_recv, late_send, late_recv, send_sem, recv_sem,
+    xrecv_d, xrecv_v, edge_v, early_send, early_recv, late_send, late_recv, send_sem, recv_sem,
 ):
     names = ("gx", "gy", "gz")
     count = part.shape[1]
@@ -547,9 +555,11 @@
     others = [d for d in DIRS if d[1] != 0]
 
     def x_messages(kind):
-        acc, recv = (acc_v, xrecv_v) if kind else (acc_d, xrecv_d)
+        src = (edge_v, acc_v.at[24:32]) if kind else (acc_d, acc_d)
+        recv = xrecv_v if kind else xrecv_d
         base = 16 + 2 * kind
-        return [copy_to(base + d, base + 1 - d, acc, recv.at[1 - d], {"gx": place[0] + 2 * d - 1}) for d in range(2)]
+        return [
+            copy_to(base + d, base + 1 - d, src[d], recv.at[1 - d], {"gx": place[0] + 2 * d - 1}) for d in range(2)]
 
     def x_start(kind):
         for (exists, _), copy in zip(ahead, x_messages(kind)):
@@ -638,6 +648,7 @@
     land_y(1, acc_v, yrecv_v, has)
     arrive(1, others)
     land_z(1, acc_v, zrecv_v, erecv_v, zin, has)
+    pack_edge(acc_v, edge_v)
     x_start(1)
     x_arrive(0)
     full = build_full(acc_d, xrecv_d.at[0], xrecv_d.at[1], has_low[0], has_high[0])
@@ -736,7 +747,9 @@
             *two(2, ROWS, FACE[1]),
             *two(2, 8, ZF),
             *two(4, 8, FACE[1]),
-            *two(2, ROWS, LW),
+            pltpu.VMEM((2, ROWS, LW), f32),
+            pltpu.VMEM((2, 8, LW), f32),
+            pltpu.VMEM((8, LW), f32),
             *two(EARLY * 8, LANE),
             *two(LATE * 8, LANE),
             pltpu.SemaphoreType.DMA((22,)),

time: 18.6 us -> 18.2 us (0.978)
  Pallas kernels: 17.1 us -> 16.8 us
    pallas_call x1, Pallas kernels: 16.3 us -> 16 us  [per_device(): pl.pallas_call(functools.partial(step_kernel, sizes), name='step', out_sh...]
where the time goes in v5:
time: 18.2 us; the launch traced here: 18.1 us
  Pallas kernels  16.8 us (92%)
  between operations  1.29 us (7%)
    pallas_call x1, Pallas kernels, per_device(): pl.pallas_call(functools.partial(step_kernel, sizes), name='step', out_sh...  16 us
    pallas_call x1, Pallas kernels, per_device(): pl.pallas_call(place_kernel, name='place', out_shape=(jax.ShapeDtypeStruc...  0.8 us

profile of v5, /device:TPU:0, one launch (start us, length us, event | category | flops | bytes accessed | tf_op | source)
XLA Modules:
  0.0 18.1 jit_solution(3330391166743035893)
XLA Ops:
  1.3 16.0 %step.1 = (f32[28,4096]{1,0:T(8,128)S(1)}, s32[8,128]{1,0:T(8,128)S(1)}, f32[8,16,32]{2,1,0:T(8,128)S(1)}) custom-call(f32[28,2048]{1,0:T(8,128)} %refs_0_.1, s32[3,2048]{1,0:T(4,128)} %refs_1_.1, f32[8,2048]{1,0:T(8,128)} %refs_2_.1, f32[24,2048]{1,0:T(8,128)} %bitcast.1, s32[1]{0:T(128)S(6)} %copy.7.refs_4_), custom_call_target="tpu_custom_call" | custom-call | tf_op jit(solution)/shard_map/step/pallas_call | solution.py:718
  17.3 0.8 %place.1 = (f32[28,3072]{1,0:T(8,128)}, f32[8,16,32]{2,1,0:T(8,128)}) custom-call(f32[28,4096]{1,0:T(8,128)S(1)} %get-tuple-element.5.ext, s32[8,128]{1,0:T(8,128)S(1)} %get-tuple-element.6.prior_ref, f32[8,16,32]{2,1,0:T(8,128)S(1)} %get-tuple-element.7.damage_in), custom_call_target="tpu_custom_call" | custom-call | tf_op jit(solution)/shard_map/place/pallas_call | solution.py:762

commit v6 on v5

--- a/solution.py
+++ b/solution.py
@@ -44,7 +44,7 @@
 WIDE = {0: KEEP, 1: 2}
 FACE = {0: up_to(KEEP * SZ, LANE), 1: up_to(2 * SZ, LANE)}
 ZA, ZB = (H - 1) * SZ // LANE * LANE, up_to((H + CY + 1) * SZ, LANE)
-FL = EX * 16
+FD = 64
 TAIL = MOST * BIN
 PARTS = 28
 SLOT = 32
@@ -304,7 +304,7 @@
     return out
 
 
-def relax_all(place, nodes, full, line):
+def relax_start(place, nodes, full):
     ix, iy, iz = place
     z, y = lane_z(1)
     gz = z - H + (iz * CZ).astype(jnp.float32)
@@ -321,6 +321,11 @@
     keep = (1.0 - relax_rate * (6.0 * length_sq + 1.0)) * inside - (2.0 * relax_rate) * drive
     push = (2.0 * relax_rate) * drive
     spread = (relax_rate * length_sq) * inside
+    return factor, damage, keep, push, spread
+
+
+def relax_all(coefficients, line):
+    _, damage, keep, push, spread = coefficients
     tiles = LW // LANE
     line[0:8, :] = jnp.zeros((8, LANE), jnp.float32)
     line[8 + tiles * RD :, :] = jnp.zeros((8, LANE), jnp.float32)
@@ -334,7 +339,7 @@
         damage = spread * ring + keep * damage + push
     for j in range(tiles):
         line[8 + j * RD : 8 + (j + 1) * RD, :] = damage[:, j * LANE : (j + 1) * LANE]
-    return damage, factor
+    return damage
 
 
 def show_damage(line, damage_out):
@@ -343,42 +348,47 @@
         damage_out[:, y, :] = pltpu.roll(own, LW - (H + y) * SZ - H, 1)[:, :CZ]
 
 
-def make_fields(damage, factor, acc, low, high, has_low, has_high, field_left):
+def velocity_field(factor, acc, low, high, has_low, has_high, field):
     row = iota((8, LW), 0)
-    last = acc[24:32, :]
     low_last = only(has_low, low[...])
-    last = last + only(has_high, high[...])
-    velocity = []
-    for c in range(3):
-        at = slice(8 * c, 8 * c + 8)
-        first = acc[at, :] + tail_rows(low_last, c)
-        velocity.append(first * factor[8:16])
-    pair = lambda v: jnp.where(row < 4, jnp.broadcast_to(v[16:17], row.shape), jnp.broadcast_to(v[17:18], row.shape))
-    last = jnp.where(row < 3, last, pltpu.roll(last, 1, 0))
-    last = jnp.where((row == 3) | (row == 7), pair(damage), last * pair(factor))
-    whole = jnp.concatenate(velocity + [damage[8:16], last], axis=0)
-    whole = pltpu.roll(whole, LW - OFF, 1)[:, :NB]
+    last = acc[24:32, :] + only(has_high, high[...])
+    velocity = [(acc[8 * c : 8 * c + 8, :] + tail_rows(low_last, c)) * factor[8:16] for c in range(3)]
+    spread = lambda r: jnp.broadcast_to(factor[r : r + 1], row.shape)
+    last = last * jnp.where(row < 3, spread(16), jnp.where(row < 6, spread(17), 0.0))
+    whole = pltpu.roll(jnp.concatenate(velocity + [last], axis=0), LW - OFF, 1)[:, :NB]
     turned = [whole, pltpu.roll(whole, NB - 1, 1)]
     for bc in range(4):
         moved = turned[bc & 1]
         if bc >> 1:
             moved = pltpu.roll(moved, NB - SZ, 1)
         for j in range(JB):
-            lanes = slice(j * LANE, (j + 1) * LANE)
-            for f in range(4):
-                field_left[pl.ds(j * FL + 4 * f + bc, 8, stride=16), :] = moved[8 * f : 8 * f + 8, lanes]
-            field_left[pl.ds(j * FL + 128 + bc, 8, stride=4), :] = moved[32:40, lanes]
-
-
-def corners(half, base_ref, field_left, got_ref, bx_ref):
+            at, lanes = j * LEFT + bc, slice(j * LANE, (j + 1) * LANE)
+            for c in range(3):
+                field[pl.ds(at + 4 * c, 8, stride=12), :] = moved[8 * c : 8 * c + 8, lanes]
+            field[pl.ds(at + 96, 8, stride=4), :] = moved[24:32, lanes]
+
+
+def damage_field(damage, field):
+    whole = pltpu.roll(damage[8:24], LW - OFF, 1)[:, :NB]
+    turned = [whole, pltpu.roll(whole, NB - 1, 1)]
+    for bc in range(4):
+        moved = turned[bc & 1]
+        if bc >> 1:
+            moved = pltpu.roll(moved, NB - SZ, 1)
+        for j in range(JB):
+            for part in range(2):
+                field[pl.ds(j * FD + 32 * part + bc, 8, stride=4), :] = (
+                    moved[8 * part : 8 * part + 8, j * LANE : (j + 1) * LANE])
+
+
+def near_nodes(half, rows, base_ref, field, got_ref):
     depth = NB // MX
     tiles = TAIL // MX
 
     def multiply(*accs):
         for k in range(depth):
-            value = jnp.concatenate(
-                [field_left[j * FL : (j + 1) * FL, :] for j in range(k * MX // LANE, (k + 1) * MX // LANE)], axis=1)
-            high, low = split(value)
+            high, low = split(jnp.concatenate(
+                [field[j * rows : (j + 1) * rows, :] for j in range(k * MX // LANE, (k + 1) * MX // LANE)], axis=1))
             for n in range(tiles):
                 at = half * TAIL + n * MX
                 pltpu.matmul_push_rhs(onehot(base_ref[:, at : at + MX], k * MX), n // 2 % 2, n % 2)
@@ -387,19 +397,22 @@
         for n in range(tiles):
             value = pltpu.matmul_pop(accs[n])
             for j in range(MX // LANE):
-                for r in range(0, FL, 8):
+                for r in range(0, rows, 8):
                     got_ref[pl.ds(r * MOST + n * MX // LANE + j, 8, stride=MOST), :] = (
                         value[r : r + 8, j * LANE : (j + 1) * LANE])
 
-    pl.run_scoped(multiply, *[pltpu.ACC(n % 2)((FL, MX), jnp.float32) for n in range(tiles)])
+    pl.run_scoped(multiply, *[pltpu.ACC(n % 2)((rows, MX), jnp.float32) for n in range(tiles)])
+
+
+def corners(half, got_ref, fields, bx_ref):
     bx = bx_ref[MOST * half : MOST * half + MOST, :]
     at = [bx == x for x in range(CX + 1)]
-    out = [[None] * 8 for _ in range(4)]
-    for f in range(4):
+    out = [[None] * 8 for _ in range(fields)]
+    for f in range(fields):
         for bc in range(4):
             near = [jnp.zeros((MOST, LANE), jnp.float32)] * 2
             for x in range(EX):
-                r = 16 * x + 4 * f + bc
+                r = 4 * (fields * x + f) + bc
                 value = got_ref[r * MOST : (r + 1) * MOST, :]
                 if x < EX - 1:
                     near[0] = jnp.where(at[x], value, near[0])
@@ -418,14 +431,17 @@
 def move(corner, w, g, p):
     moved = [total([w(k) * corner[i][k] for k in range(8)]) for i in range(3)]
     velgrad = [[total([corner[i][k] * g(j, k) for k in range(8)]) for j in range(3)] for i in range(3)]
-    damaged = jnp.maximum(p(23), total([w(k) * corner[3][k] for k in range(8)]))
     deform = [[p(5 + 3 * i + j) for j in range(3)] for i in range(3)]
     stretch = [[(1.0 if i == j else 0.0) + time_step * velgrad[i][j] for j in range(3)] for i in range(3)]
     mapped = [
         stretch[i][0] * deform[0][j] + stretch[i][1] * deform[1][j] + stretch[i][2] * deform[2][j]
         for i in range(3) for j in range(3)
     ]
-    return moved + mapped + [damaged]
+    return moved + mapped
+
+
+def damage_of(corner, w, p):
+    return [jnp.maximum(p(23), total([w(k) * corner[0][k] for k in range(8)]))]
 
 
 def finish(late, early):
@@ -464,7 +480,7 @@
 
 def step_body(
     accs, sizes, part_in, base_in, weight_in, slope_in, counts, ext, prior_out, damage_out,
-    part, base_ref, weight, slope, load_sem, out, sums, acc_d, acc_v, zin, line, field_left, got, turned, bx_ref,
+    part, base_ref, weight, slope, load_sem, out, sums, acc_d, acc_v, zin, line, field_v, field_d, got_v, got_d, turned, bx_ref,
     ysend_d, yrecv_d, zsend_d, zrecv_d, esend_d, erecv_d, ysend_v, yrecv_v, zsend_v, zrecv_v, esend_v, erecv_v,
     xrecv_d, xrecv_v, edge_v, early_send, early_recv, late_send, late_recv, send_sem, recv_sem,
 ):
@@ -651,11 +667,21 @@
     pack_edge(acc_v, edge_v)
     x_start(1)
     x_arrive(0)
+    x_arrive(1)
     full = build_full(acc_d, xrecv_d.at[0], xrecv_d.at[1], has_low[0], has_high[0])
     nodes = [n * c for n, c in zip(sizes, (CX, CY, CZ))]
-    damage, factor = relax_all(place, nodes, full, line)
-    x_arrive(1)
-    make_fields(damage, factor, acc_v, xrecv_v.at[0], xrecv_v.at[1], has_low[0], has_high[0], field_left)
+    coefficients = relax_start(place, nodes, full)
+    tail_half = bins // MOST - 1
+    velocity_field(
+        coefficients[0], acc_v, xrecv_v.at[0], xrecv_v.at[1], has_low[0], has_high[0], field_v)
+    near_nodes(tail_half, LEFT, base_ref, field_v, got_v)
+    w, g, p = dense(tail_half)
+    tail_late = move(corners(tail_half, got_v, 3, bx_ref), w, g, p)
+    damage = relax_all(coefficients, line)
+    for q, value in enumerate(tail_late):
+        late_send[8 * q : 8 * q + 8, :] = value
+    flying.append(ring(21, late_send.at[: 8 * LATE - 8], late_recv.at[: 8 * LATE - 8]))
+    damage_field(damage, field_d)
 
     def store(first, values, gone=None):
 
@@ -671,12 +697,17 @@
 
     for half in reversed(range(halves)):
         w, g, p = dense(half)
-        late = move(corners(half, base_ref, field_left, got, bx_ref), w, g, p)
+        if half != tail_half:
+            near_nodes(half, LEFT, base_ref, field_v, got_v)
+            late = move(corners(half, got_v, 3, bx_ref), w, g, p)
+        else:
+            late = tail_late
+        near_nodes(half, FD, base_ref, field_d, got_d)
+        late = late + damage_of(corners(half, got_d, 1, bx_ref), w, p)
         gone = None
         if half == halves - 1:
-            for q, value in enumerate(late):
-                late_send[8 * q : 8 * q + 8, :] = value
-            flying.append(ring(21, late_send, late_recv))
+            late_send[8 * LATE - 8 :, :] = late[-1]
+            flying.append(ring(22, late_send.at[8 * LATE - 8 :], late_recv.at[8 * LATE - 8 :]))
             show_damage(line, damage_out)
             gone = iota((MOST, LANE), 0) + jnp.broadcast_to(counts[0], (MOST, LANE)) >= MOST
         store((half + 1) * MOST, finish(late, [p(0), p(1), p(24), p(25), p(26), p(27)]), gone)
@@ -737,8 +768,10 @@
             pltpu.VMEM((ROWS, LW), f32),
             pltpu.VMEM((8, LW), f32),
             pltpu.VMEM((16 + LW // LANE * RD, LANE), f32),
-            pltpu.VMEM((JB * FL, LANE), f32),
-            pltpu.VMEM((MOST * FL, LANE), f32),
+            pltpu.VMEM((JB * LEFT, LANE), f32),
+            pltpu.VMEM((JB * FD, LANE), f32),
+            pltpu.VMEM((MOST * LEFT, LANE), f32),
+            pltpu.VMEM((MOST * FD, LANE), f32),
             pltpu.VMEM((GROUPS * bins * 8, LANE), f32),
             pltpu.VMEM((bins, LANE), jnp.int32),
             *two(2, ROWS, FACE[0]),
@@ -752,8 +785,8 @@
             pltpu.VMEM((8, LW), f32),
             *two(EARLY * 8, LANE),
             *two(LATE * 8, LANE),
-            pltpu.SemaphoreType.DMA((22,)),
-            pltpu.SemaphoreType.DMA((22,)),
+            pltpu.SemaphoreType.DMA((23,)),
+            pltpu.SemaphoreType.DMA((23,)),
         ],
         compiler_params=pltpu.CompilerParams(
             collective_id=0, has_side_effects=True, vmem_limit_bytes=60 * 1024 * 1024

time: 18.2 us -> 17.6 us (0.967)
  Pallas kernels: 16.8 us -> 16.1 us
    pallas_call x1, Pallas kernels: 16 us -> 15.3 us  [per_device(): pl.pallas_call(functools.partial(step_kernel, sizes), name='step', out_sh...]
where the time goes in v6:
time: 17.6 us; the launch traced here: 17.4 us
  Pallas kernels  16.1 us (91%)
  between operations  1.29 us (7%)
    pallas_call x1, Pallas kernels, per_device(): pl.pallas_call(functools.partial(step_kernel, sizes), name='step', out_sh...  15.3 us
    pallas_call x1, Pallas kernels, per_device(): pl.pallas_call(place_kernel, name='place', out_shape=(jax.ShapeDtypeStruc...  0.8 us

profile of v6, /device:TPU:0, one launch (start us, length us, event | category | flops | bytes accessed | tf_op | source)
XLA Modules:
  0.0 17.4 jit_solution(11484816890068651200)
XLA Ops:
  1.3 15.3 %step.1 = (f32[28,4096]{1,0:T(8,128)S(1)}, s32[8,128]{1,0:T(8,128)S(1)}, f32[8,16,32]{2,1,0:T(8,128)S(1)}) custom-call(f32[28,2048]{1,0:T(8,128)} %refs_0_.1, s32[3,2048]{1,0:T(4,128)} %refs_1_.1, f32[8,2048]{1,0:T(8,128)} %refs_2_.1, f32[24,2048]{1,0:T(8,128)} %bitcast.1, s32[1]{0:T(128)S(6)} %copy.7.refs_4_), custom_call_target="tpu_custom_call" | custom-call | tf_op jit(solution)/shard_map/step/pallas_call | solution.py:749
  16.6 0.8 %place.1 = (f32[28,3072]{1,0:T(8,128)}, f32[8,16,32]{2,1,0:T(8,128)}) custom-call(f32[28,4096]{1,0:T(8,128)S(1)} %get-tuple-element.5.ext, s32[8,128]{1,0:T(8,128)S(1)} %get-tuple-element.6.prior_ref, f32[8,16,32]{2,1,0:T(8,128)S(1)} %get-tuple-element.7.damage_in), custom_call_target="tpu_custom_call" | custom-call | tf_op jit(solution)/shard_map/place/pallas_call | solution.py:795

commit v7 on v6

--- a/solution.py
+++ b/solution.py
@@ -652,7 +652,6 @@
     early.append(jnp.broadcast_to(counts[0], (8, LANE)).astype(jnp.float32))
     for q, value in enumerate(early):
         early_send[8 * q : 8 * q + 8, :] = value
-    flying.append(ring(20, early_send, early_recv))
     ext[:, (MOST + bins) * LANE :] = jnp.zeros((PARTS, TAIL), jnp.float32)
 
     arrive(0, faces_y)
@@ -660,6 +659,7 @@
     arrive(0, others)
     land_z(0, acc_d, zrecv_d, erecv_d, zin, has)
     x_start(0)
+    flying.append(ring(20, early_send, early_recv))
     arrive(1, faces_y)
     land_y(1, acc_v, yrecv_v, has)
     arrive(1, others)

time: 17.6 us -> 17.6 us (level)
  no operation moved by 1% of the time
where the time goes in v7:
time: 17.6 us; the launch traced here: 17.4 us
  Pallas kernels  16.1 us (91%)
  between operations  1.29 us (7%)
    pallas_call x1, Pallas kernels, per_device(): pl.pallas_call(functools.partial(step_kernel, sizes), name='step', out_sh...  15.3 us
    pallas_call x1, Pallas kernels, per_device(): pl.pallas_call(place_kernel, name='place', out_shape=(jax.ShapeDtypeStruc...  0.8 us

profile of v7, /device:TPU:0, one launch (start us, length us, event | category | flops | bytes accessed | tf_op | source)
XLA Modules:
  0.0 17.4 jit_solution(5800091551662236276)
XLA Ops:
  1.3 15.3 %step.1 = (f32[28,4096]{1,0:T(8,128)S(1)}, s32[8,128]{1,0:T(8,128)S(1)}, f32[8,16,32]{2,1,0:T(8,128)S(1)}) custom-call(f32[28,2048]{1,0:T(8,128)} %refs_0_.1, s32[3,2048]{1,0:T(4,128)} %refs_1_.1, f32[8,2048]{1,0:T(8,128)} %refs_2_.1, f32[24,2048]{1,0:T(8,128)} %bitcast.1, s32[1]{0:T(128)S(6)} %copy.7.refs_4_), custom_call_target="tpu_custom_call" | custom-call | tf_op jit(solution)/shard_map/step/pallas_call | solution.py:749
  16.6 0.8 %place.1 = (f32[28,3072]{1,0:T(8,128)}, f32[8,16,32]{2,1,0:T(8,128)}) custom-call(f32[28,4096]{1,0:T(8,128)S(1)} %get-tuple-element.5.ext, s32[8,128]{1,0:T(8,128)S(1)} %get-tuple-element.6.prior_ref, f32[8,16,32]{2,1,0:T(8,128)S(1)} %get-tuple-element.7.damage_in), custom_call_target="tpu_custom_call" | custom-call | tf_op jit(solution)/shard_map/place/pallas_call | solution.py:795
